TPU v7x, 256 devices: a whole 4x4x8 slice. The times are simulated.
256 devices in a mesh: row: 16 (over z_hi, y, core), col: 16 (over x, z_lo).
Axes of the slice: x: 4, y: 4, z: 8 (z_hi: 2, z_lo: 4; z = z_hi * 4 + z_lo), core: 2. Of those that a mesh axis runs over, the one named last changes fastest.
Arguments:
- features: bfloat16 [65536, 256], P(('col', 'row')), may hold values from -6 to 6
- adj_tiles: bfloat16 [16, 16, 80, 256, 256], P('row', 'col'), may hold values from -0.078125 to 0.078125
- tile_rows: int32 [16, 16, 80], P('row', 'col'), may hold values from 0 to 15, as said below
- tile_cols: int32 [16, 16, 80], P('row', 'col'), may hold values from 0 to 15, as said below
- tile_count: int32 [16, 16], P('row', 'col'), may hold values from 1 to 80, as said below
- weight: bfloat16 [256, 256], replicated, may hold values from -0.375 to 0.375
- grad_out: bfloat16 [65536, 256], P(('row', 'col')), may hold values from -6 to 6
Outputs:
- activation: bfloat16 [65536, 256], P(('row', 'col'))
- weight_grad: float32 [256, 256], replicated
- x_grad: bfloat16 [65536, 256], P(('col', 'row'))
Inputs may be any that keep to these rules, and one draw needn't show every extreme that they name: On each grid block the 80 slots name distinct tile positions (tile_rows, tile_cols). `tile_cols`: paired with tile_rows slot by slot. `tile_count`: slots of a grid block at or beyond its count are ignored.
All inputs are finite; a program needn't handle non-finite values.
Results may differ from a plain program's by a relative error of at most 0.025.
Values may be sent and summed in bfloat16 or wider, within the bound.
No kernel may reach another device: no remote copies, remote signals or barrier semaphores. Data moves between devices by JAX's collectives and lax.ppermute only.
A program may use at most 128 MiB of HBM per device.

v0:
```python
import math

import jax
import jax.numpy as jnp
from jax import lax
from jax.sharding import PartitionSpec as P


def local(features, adj_tiles, tile_rows, tile_cols, tile_count, weight, grad_out):
    blocks = adj_tiles[0, 0]
    row_ids = tile_rows[0, 0]
    col_ids = tile_cols[0, 0]
    tile_total = tile_count[0, 0]
    slot_total = blocks.shape[0]
    tile_edge = blocks.shape[1]
    group_size = min(8, slot_total)
    feat_width = features.shape[1]
    local_rows = features.shape[0]
    row_devices = lax.axis_size("row")
    col_devices = lax.axis_size("col")
    row_tiles = local_rows * col_devices // tile_edge
    col_tiles = local_rows * row_devices // tile_edge
    group_count = (tile_total + group_size - 1) // group_size
    lanes = jnp.arange(group_size, dtype=jnp.int32)
    gathered = lax.all_gather(features, "row", axis=0, tiled=True).reshape(
        -1, tile_edge, feat_width
    )

    def forward_group(group_index, running):
        offset = group_index * group_size
        block_tiles = lax.dynamic_slice_in_dim(blocks, offset, group_size, 0)
        group_rows = lax.dynamic_slice_in_dim(row_ids, offset, group_size, 0)
        group_cols = lax.dynamic_slice_in_dim(col_ids, offset, group_size, 0)
        active = (offset + lanes < tile_total).astype(jnp.float32)
        product = jnp.einsum(
            "gij,gjf->gif", block_tiles, gathered[group_cols], preferred_element_type=jnp.float32
        )
        return running.at[group_rows].add(product * active[:, None, None])

    partial_rows = lax.fori_loop(
        0, group_count, forward_group, jnp.zeros((row_tiles, tile_edge, feat_width), jnp.float32)
    )
    partial_rows = partial_rows.reshape(-1, feat_width)
    node_total = local_rows * row_devices * col_devices
    grad_scale = 1.0 / math.sqrt(node_total)
    contract_rows = (((0,), (0,)), ((), ()))
    aggregated = lax.psum_scatter(
        partial_rows.astype(jnp.bfloat16), "col", scatter_dimension=0, tiled=True
    )
    pre_act = jnp.dot(aggregated, weight, preferred_element_type=jnp.float32)
    gate_sig = jax.nn.sigmoid(pre_act)
    activation = (pre_act * gate_sig).astype(jnp.bfloat16)
    silu_slope = gate_sig * (1.0 + pre_act * (1.0 - gate_sig))
    act_grad = (grad_out.astype(jnp.float32) * silu_slope).astype(jnp.bfloat16)
    weight_term = lax.dot_general(
        aggregated, act_grad, contract_rows, preferred_element_type=jnp.float32
    )
    weight_total = lax.psum(weight_term, ("row", "col"))
    msg_grad = jnp.dot(act_grad, weight.T, preferred_element_type=jnp.float32).astype(jnp.bfloat16)
    msg_block = lax.all_gather(msg_grad, "col", axis=0, tiled=True)
    weight_grad = weight_total * grad_scale
    msg_tiles = msg_block.reshape(-1, tile_edge, feat_width)

    def backward_group(group_index, running):
        offset = group_index * group_size
        block_tiles = lax.dynamic_slice_in_dim(blocks, offset, group_size, 0)
        group_rows = lax.dynamic_slice_in_dim(row_ids, offset, group_size, 0)
        group_cols = lax.dynamic_slice_in_dim(col_ids, offset, group_size, 0)
        active = (offset + lanes < tile_total).astype(jnp.float32)
        product = jnp.einsum(
            "gij,gif->gjf", block_tiles, msg_tiles[group_rows], preferred_element_type=jnp.float32
        )
        return running.at[group_cols].add(product * active[:, None, None])

    grad_part = lax.fori_loop(
        0, group_count, backward_group, jnp.zeros((col_tiles, tile_edge, feat_width), jnp.float32)
    )
    grad_part = grad_part.reshape(-1, feat_width)
    x_grad = lax.psum_scatter(
        grad_part.astype(jnp.bfloat16), "row", scatter_dimension=0, tiled=True
    )
    return (activation, weight_grad, x_grad)


def solution(mesh):
    return jax.shard_map(
        local,
        mesh=mesh,
        in_specs=(
            P(("col", "row"), None),
            P("row", "col", None, None, None),
            P("row", "col", None),
            P("row", "col", None),
            P("row", "col"),
            P(),
            P(("row", "col"), None),
        ),
        out_specs=(P(("row", "col"), None), P(), P(("col", "row"), None)),
        check_vma=False,
    )
```

profile of v0, /device:TPU:2, one launch (start us, length us, event | category | flops | bytes accessed | tf_op | source)
XLA Modules:
  0.0 696.0 jit_solution(8350627286856885725)
XLA Ops:
  7.2 0.0 copy-start
  7.2 0.0 copy-start.3
  7.2 0.0 copy-start.2
  7.2 0.0 all-gather.3.cloned.1.call-start
  7.2 0.7 all-gather.3.cloned.1.call-update
  7.9 0.0 reduce-scatter.3.cloned.1.call-start
  8.6 68.1 %all-gather.3.cloned.1.call-done = bf16[4096,256]{1,0:T(8,128)(2,1)} async-done(((bf16[256,256]{1,0:T(8,128)(2,1)}), bf16[4096,256]{1,0:T(8,128)(2,1)}) %all-gather.3.cloned.1.call-update) | async-done | bytes 2097168 | tf_op jit(solution)/shard_map/all_gather | solution.py:25
  76.7 2.4 broadcast.35.clone
  79.1 0.0 copy-done.3
  79.1 0.0 copy-done.2
  79.1 26.9 %while.22 = (s32[]{:T(128)}, f32[16,256,256]{2,1,0:T(8,128)}, s32[]{:T(128)}, s32[80]{0:T(128)S(1)}, bf16[80,256,256]{2,1,0:T(8,128)(2,1)}, /*index=5*/s32[80]{0...) while((s32[]{:T(128)}, f32[16,256,256]{2,1,0:T(8,128)}, ...), condition=%wide.region_2.3_spmd.clone, body=%wide.region_0.2_spmd.clone.sunk | while | flops 269485120 | bytes 12587475 | solution.py:40
  79.1 0.6 compare_convert_fusion.4
  79.8 0.1 compare_select_fusion.6
  79.9 2.2 gather_fusion
  82.1 1.7 convolution_multiply_fusion.4
  83.7 4.3 scatter_fusion
  88.0 0.6 compare_convert_fusion.4
  88.7 0.1 compare_select_fusion.6
  88.8 2.2 gather_fusion
  91.0 1.7 convolution_multiply_fusion.4
  92.7 4.3 scatter_fusion
  97.0 0.6 compare_convert_fusion.4
  97.7 0.1 compare_select_fusion.6
  97.8 2.2 gather_fusion
  100.0 1.7 convolution_multiply_fusion.4
  101.6 4.3 scatter_fusion
  106.0 3.8 convert_element_type.38
  109.8 0.0 reduce-scatter.3.cloned.1.call-update
  109.8 0.0 all-gather.5.cloned.1.call-start
  109.9 139.6 %reduce-scatter.3.cloned.1.call-done = bf16[256,256]{1,0:T(8,128)(2,1)} async-done(((bf16[4096,256]{1,0:T(8,128)(2,1)}), bf16[256,256]{1,0:T(8,128)(2,1)}) %reduce-scatter.3.cloned.1.call-update) | async-done | bytes 131088 | tf_op jit(solution)/shard_map/reduce_scatter | solution.py:47
  249.5 0.0 copy-done
  249.5 0.0 copy-done.4
  249.5 1.8 multiply_convert_fusion
  251.4 0.9 convolution_convert_fusion
  252.2 0.0 all-gather.5.cloned.1.call-update
  252.3 0.0 all-reduce.2.cloned.1.call-start
  252.3 14.4 %copy.10 = bf16[1,1,80,256,256]{3,4,2,1,0:T(8,128)(2,1)} copy(bf16[1,1,80,256,256]{4,3,2,1,0:T(8,128)(2,1)} %bitcast.23) | data formatting | bytes 20971520 | tf_op args[1]
  266.8 0.0 copy-done.1
  266.8 0.9 fusion.8
  267.7 0.0 all-reduce.2.cloned.1.call-update
  267.7 0.0 reduce-scatter.5.cloned.1.call-start
  267.8 68.7 %all-gather.5.cloned.1.call-done = bf16[4096,256]{1,0:T(8,128)(2,1)} async-done(((bf16[256,256]{1,0:T(8,128)(2,1)}), bf16[4096,256]{1,0:T(8,128)(2,1)}) %all-gather.5.cloned.1.call-update) | async-done | bytes 2097168 | tf_op jit(solution)/shard_map/all_gather | solution.py:60
  336.5 2.5 broadcast.35
  339.0 26.8 %while.23 = (s32[]{:T(128)}, f32[16,256,256]{2,1,0:T(8,128)}, s32[]{:T(128)}, s32[80]{0:T(128)S(1)}, bf16[80,256,256]{1,2,0:T(8,128)(2,1)}, /*index=5*/s32[80]{0...) while((s32[]{:T(128)}, f32[16,256,256]{2,1,0:T(8,128)}, ...), condition=%wide.region_7.8_spmd.clone, body=%wide.region_5.7_spmd.clone.sunk | while | flops 269485120 | bytes 12587475 | solution.py:75
  339.0 0.6 compare_convert_fusion.5
  339.7 0.1 compare_select_fusion.7
  339.8 2.2 gather_fusion.1
  342.0 1.7 convolution_multiply_fusion.5
  343.7 4.3 scatter_fusion.1
  347.9 0.6 compare_convert_fusion.5
  348.6 0.1 compare_select_fusion.7
  348.7 2.2 gather_fusion.1
  350.9 1.7 convolution_multiply_fusion.5
  352.6 4.2 scatter_fusion.1
  356.8 0.6 compare_convert_fusion.5
  357.4 0.1 compare_select_fusion.7
  357.5 2.2 gather_fusion.1
  359.7 1.7 convolution_multiply_fusion.5
  361.4 4.4 scatter_fusion.1
  365.8 3.8 convert_element_type.44
  369.6 0.0 reduce-scatter.5.cloned.1.call-update
  369.7 229.0 %all-reduce.2.cloned.1.call-done = f32[256,256]{1,0:T(8,128)} async-done(((f32[256,256]{1,0:T(8,128)}), f32[256,256]{1,0:T(8,128)}) %all-reduce.2.cloned.1.call-update) | async-done | bytes 262160 | tf_op jit(solution)/shard_map/psum | solution.py:58
  598.7 1.7 broadcast_multiply_fusion
  600.3 89.1 %reduce-scatter.5.cloned.1.call-done = bf16[256,256]{1,0:T(8,128)(2,1)} async-done(((bf16[4096,256]{1,0:T(8,128)(2,1)}), bf16[256,256]{1,0:T(8,128)(2,1)}) %reduce-scatter.5.cloned.1.call-update) | async-done | bytes 131088 | tf_op jit(solution)/shard_map/reduce_scatter | solution.py:79
  (8 shorter events, 0.0 us)
Async XLA Ops:
  7.2 242.3 %copy-start = (bf16[256,256]{1,0:T(8,128)(2,1)S(1)}, bf16[256,256]{1,0:T(8,128)(2,1)}, u32[]{:S(2)}) copy-start(bf16[256,256]{1,0:T(8,128)(2,1)} %param.16) | copy-start | bytes 393220
  7.2 71.9 %copy-start.3 = (s32[1,1,80]{2,1,0:T(1,128)S(1)}, s32[1,1,80]{2,1,0:T(1,128)}, u32[]{:S(2)}) copy-start(s32[1,1,80]{2,1,0:T(1,128)} %param.14) | copy-start | bytes 964
  7.2 71.9 %copy-start.2 = (s32[1,1,80]{2,1,0:T(1,128)S(1)}, s32[1,1,80]{2,1,0:T(1,128)}, u32[]{:S(2)}) copy-start(s32[1,1,80]{2,1,0:T(1,128)} %param.13) | copy-start | bytes 964
  7.2 69.5 %all-gather.3.cloned.1.call-start = ((), (), s32[]{:S(2)}) async-start(), calls=%async_computation.2 | async-start | bytes 2228224 | tf_op jit(solution)/shard_map/all_gather | solution.py:25
  7.9 241.6 %reduce-scatter.3.cloned.1.call-start = ((), (), s32[]{:S(2)}) async-start(), calls=%async_computation.3 | async-start | bytes 2228224 | tf_op jit(solution)/shard_map/reduce_scatter | solution.py:47
  106.0 143.5 %copy-start.4 = (bf16[256,256]{1,0:T(8,128)(2,1)S(1)}, bf16[256,256]{1,0:T(8,128)(2,1)}, u32[]{:S(2)}) copy-start(bf16[256,256]{1,0:T(8,128)(2,1)} %param.17) | copy-start | bytes 393220
  109.8 226.7 %all-gather.5.cloned.1.call-start = ((), (), s32[]{:S(2)}) async-start(), calls=%async_computation.5 | async-start | bytes 2228224 | tf_op jit(solution)/shard_map/all_gather | solution.py:60
  252.3 346.4 %all-reduce.2.cloned.1.call-start = ((), (), s32[]{:S(2)}) async-start(), calls=%async_computation.4 | async-start | bytes 524288 | tf_op jit(solution)/shard_map/psum | solution.py:58
  252.3 14.5 %copy-start.1 = (bf16[256,256]{1,0:T(8,128)(2,1)S(1)}, bf16[256,256]{1,0:T(8,128)(2,1)}, u32[]{:S(2)}) copy-start(bf16[256,256]{1,0:T(8,128)(2,1)} %reduce-scatter.3.cloned.1.call-done) | copy-start | bytes 393220
  267.7 421.7 %reduce-scatter.5.cloned.1.call-start = ((), (), s32[]{:S(2)}) async-start(), calls=%async_computation.6 | async-start | bytes 2228224 | tf_op jit(solution)/shard_map/reduce_scatter | solution.py:79
Sparse Core Ops, SparseCore 0:
  10.8 65.9 all-gather.2
  109.9 139.5 reduce-scatter.2
  252.4 84.0 all-gather.4
  342.4 256.2 all-reduce.1
  603.3 86.0 reduce-scatter.4
where the time goes:
time: 699 us; the launch traced here: 696 us
  waiting for transfers between devices  595 us (85%)
  other arithmetic  39.5 us (6%)
  local copies, waits for them, and re-layouts  32.6 us (5%)
  between operations  14.5 us (2%)
  matrix products  13.7 us (2%)
    psum x1, waiting for transfers between devices, local(): weight_total = lax.psum(weight_term, ('row', 'col'))  229 us
    reduce_scatter x1, waiting for transfers between devices, local(): lax.psum_scatter(partial_rows.astype(jnp.bfloat16), 'col', scatter_dimens...  140 us
    reduce_scatter x1, waiting for transfers between devices, local(): lax.psum_scatter(grad_part.astype(jnp.bfloat16), 'row', scatter_dimension...  89.1 us
    all_gather x1, waiting for transfers between devices, local(): msg_block = lax.all_gather(msg_grad, 'col', axis=0, tiled=True)  68.7 us
    all_gather x1, waiting for transfers between devices, local(): lax.all_gather(features, 'row', axis=0, tiled=True)  68.1 us
    unnamed x11, local copies, waits for them, and re-layouts  14.5 us
  transfers between devices with their start and end apart: 5, of which 5 were waited for; matrix products, arithmetic and copies ran while one was open for 7% of the time, Pallas kernels for 0%

commit v1 on v0

v1 whole, which is shorter than its diff:
```python
import functools
import math

import jax
import jax.numpy as jnp
from jax import lax
from jax.experimental import pallas as pl
from jax.experimental.pallas import tpu as pltpu
from jax.sharding import PartitionSpec as P

ROW_DEVICES = 16
COL_DEVICES = 16
UNROLL = 4
VMEM_BYTES = 60 << 20
BF16 = jnp.bfloat16
F32 = jnp.float32


def row_permute(value, zh=0, y=0, core=0):
    pairs = []
    for i in range(ROW_DEVICES):
        to_zh, to_y, to_core = (i >> 3) ^ zh, (((i >> 1) & 3) + y) % 4, (i & 1) ^ core
        pairs.append((i, (to_zh * 4 + to_y) * 2 + to_core))
    return lax.ppermute(value, "row", pairs)


def col_permute(value, x=0, zl=0):
    pairs = []
    for i in range(COL_DEVICES):
        pairs.append((i, (((i >> 2) + x) % 4) * 4 + ((i & 3) + zl) % 4))
    return lax.ppermute(value, "col", pairs)


def row_tile(k, j, flip):
    index = lax.axis_index("row")
    zh, y, core = index >> 3, (index >> 1) & 3, index & 1
    return ((zh ^ j) * 4 + ((y + k) & 3)) * 2 + (core ^ flip)


def col_tile(k, j):
    index = lax.axis_index("col")
    return (((index >> 2) + k) & 3) * 4 + ((index + j) & 3)


def tile_loop(count, into, frm, tiles, panel, tile_buf, acc, tile_sem, piece_copies, contract):
    @pl.loop(0, count)
    def _(i):
        pltpu.make_async_copy(tiles.at[i], tile_buf.at[i], tile_sem.at[i]).start()

    for copy in piece_copies:
        copy.start()

    @pl.loop(0, acc.shape[0])
    def _(i):
        acc[i] = jnp.zeros(acc.shape[1:], F32)

    for copy in piece_copies:
        copy.wait()

    def arrive(i):
        pltpu.make_async_copy(tiles.at[i], tile_buf.at[i], tile_sem.at[i]).wait()

    def product(i):
        return lax.dot_general(
            tile_buf[i], panel[frm[i]], (((contract,), (0,)), ((), ())), preferred_element_type=F32
        )

    groups = count // UNROLL

    @pl.loop(0, groups)
    def _(group):
        first = group * UNROLL
        for j in range(UNROLL):
            arrive(first + j)
        terms = [product(first + j) for j in range(UNROLL)]
        for j in range(UNROLL):
            acc[into[first + j]] += terms[j]

    @pl.loop(groups * UNROLL, count)
    def _(i):
        arrive(i)
        acc[into[i]] += product(i)


def forward_kernel(cnt, into, frm, near, far, tiles, o0, o1, o2, o3, panel, tile_buf, acc, tile_sem, piece_sem):
    copies = []
    for flip, piece in enumerate((near, far)):
        for k in range(4):
            for j in range(2):
                n = k * 2 + j
                copies.append(
                    pltpu.make_async_copy(
                        piece.at[n], panel.at[row_tile(-k, j, flip)], piece_sem.at[flip * 8 + n]
                    )
                )
    tile_loop(cnt[0], into, frm, tiles, panel, tile_buf, acc, tile_sem, copies, 1)
    for k, out in enumerate((o0, o1, o2, o3)):
        for j in range(4):
            out[j] = acc[col_tile(k, j)].astype(BF16)


def backward_kernel(cnt, into, frm, g0, g1, g2, g3, tiles, own, sent, panel, tile_buf, acc, tile_sem, piece_sem):
    copies = []
    for k, piece in enumerate((g0, g1, g2, g3)):
        for j in range(4):
            copies.append(
                pltpu.make_async_copy(
                    piece.at[j], panel.at[col_tile(-k, -j)], piece_sem.at[k * 4 + j]
                )
            )
    tile_loop(cnt[0], into, frm, tiles, panel, tile_buf, acc, tile_sem, copies, 0)
    for flip, out in enumerate((own, sent)):
        for k in range(4):
            for j in range(2):
                out[k * 2 + j] = acc[row_tile(k, j, flip)].astype(BF16)


def tile_call(kernel, name, cnt, into, frm, pieces, tiles, out_shapes):
    slots, edge, _ = tiles.shape
    smem = pl.BlockSpec(memory_space=pltpu.SMEM)
    hbm = pl.BlockSpec(memory_space=pl.ANY)
    return pl.pallas_call(
        kernel,
        out_shape=[jax.ShapeDtypeStruct(shape, BF16) for shape in out_shapes],
        in_specs=[smem] * 3 + [hbm] * (len(pieces) + 1),
        out_specs=[pl.BlockSpec(memory_space=pltpu.VMEM)] * len(out_shapes),
        scratch_shapes=[
            pltpu.VMEM((16, edge, edge), BF16),
            pltpu.VMEM((slots, edge, edge), BF16),
            pltpu.VMEM((16, edge, edge), F32),
            pltpu.SemaphoreType.DMA((slots,)),
            pltpu.SemaphoreType.DMA((16,)),
        ],
        compiler_params=pltpu.CompilerParams(vmem_limit_bytes=VMEM_BYTES),
        cost_estimate=pl.CostEstimate(
            flops=2 * slots * edge**3, bytes_accessed=slots * edge * edge * 2, transcendentals=0
        ),
        name=name,
    )(cnt, into, frm, *pieces, tiles)


def dense_kernel(own, q1, q2, q3, weight, grad_out, activation, msg_grad, weight_term):
    total = own[...] + q1[...].astype(F32) + q2[...].astype(F32) + q3[...].astype(F32)
    aggregated = total.astype(BF16)
    pre_act = jnp.dot(aggregated, weight[...], preferred_element_type=F32)
    gate_sig = 1.0 / (1.0 + jnp.exp(-pre_act))
    activation[...] = (pre_act * gate_sig).astype(BF16)
    slope = gate_sig * (1.0 + pre_act * (1.0 - gate_sig))
    act_grad = (grad_out[...].astype(F32) * slope).astype(BF16)
    weight_term[...] = lax.dot_general(
        aggregated, act_grad, (((0,), (0,)), ((), ())), preferred_element_type=F32
    )
    msg_grad[...] = lax.dot_general(
        act_grad, weight[...], (((1,), (1,)), ((), ())), preferred_element_type=F32
    ).astype(BF16)


def dense_call(own, q1, q2, q3, weight, grad_out):
    shape = grad_out.shape
    return pl.pallas_call(
        dense_kernel,
        out_shape=[
            jax.ShapeDtypeStruct(shape, BF16),
            jax.ShapeDtypeStruct(shape, BF16),
            jax.ShapeDtypeStruct(weight.shape, F32),
        ],
        cost_estimate=pl.CostEstimate(flops=6 * 256**3, bytes_accessed=10**6, transcendentals=65536),
        name="dense",
    )(own, q1, q2, q3, weight, grad_out)


def ordered_sum(pieces, position):
    stacked = jnp.stack(pieces)
    total = lax.dynamic_index_in_dim(stacked, position & 3, 0, keepdims=False)
    for place in range(1, 4):
        total = total + lax.dynamic_index_in_dim(stacked, (position - place) & 3, 0, keepdims=False)
    return total


def reduce_weight(term):
    row, col = lax.axis_index("row"), lax.axis_index("col")
    zh, y, core = row >> 3, (row >> 1) & 3, row & 1
    x, zl = col >> 2, col & 3
    width = term.shape[1]

    def part(value, index, count):
        rows = value.shape[0] // count
        return lax.dynamic_slice_in_dim(value, index * rows, rows, 0)

    half = part(term, core, 2) + row_permute(part(term, core ^ 1, 2), core=1)
    eighth = part(half, y, 4)
    for k in range(1, 4):
        eighth = eighth + row_permute(part(half, (y + k) & 3, 4), y=k)
    mine = part(eighth, zh, 2) + row_permute(part(eighth, zh ^ 1, 2), zh=1)
    mine = ordered_sum([mine] + [col_permute(mine, x=k) for k in (1, 2, 3)], x)
    mine = ordered_sum([mine] + [col_permute(mine, zl=k) for k in (1, 2, 3)], zl)
    other = row_permute(mine, zh=1)
    pair = jnp.where(zh == 0, jnp.stack([mine, other]), jnp.stack([other, mine]))
    pair = pair.reshape(-1, width)
    quads = jnp.stack([pair] + [row_permute(pair, y=k) for k in (1, 2, 3)])
    quads = jnp.stack(
        [lax.dynamic_index_in_dim(quads, (y - place) & 3, 0, keepdims=False) for place in range(4)]
    ).reshape(-1, width)
    sibling = row_permute(quads, core=1)
    whole = jnp.where(core == 0, jnp.stack([quads, sibling]), jnp.stack([sibling, quads]))
    return whole.reshape(-1, width)


def add_all(pieces):
    total = pieces[0].astype(F32)
    for piece in pieces[1:]:
        total = total + piece.astype(F32)
    return total


def local(features, adj_tiles, tile_rows, tile_cols, tile_count, weight, grad_out):
    tiles = adj_tiles[0, 0]
    row_ids, col_ids, count = tile_rows[0, 0], tile_cols[0, 0], tile_count[0]
    edge, width = features.shape
    node_total = edge * ROW_DEVICES * COL_DEVICES

    with jax.named_scope("gather_features"):
        pair = jnp.stack([features, row_permute(features, zh=1)])
        near = jnp.concatenate([pair] + [row_permute(pair, y=k) for k in (1, 2, 3)])
        far = row_permute(near, core=1)

    parts = tile_call(
        forward_kernel, "forward_tiles", count, row_ids, col_ids, [near, far], tiles, [(4, edge, width)] * 4
    )

    with jax.named_scope("reduce_aggregate"):
        parts = [parts[0]] + [col_permute(parts[k], x=k) for k in (1, 2, 3)]
        sums = [add_all([part[j] for part in parts]) for j in range(4)]
        arrived = [col_permute(sums[k].astype(BF16), zl=k) for k in (1, 2, 3)]

    activation, msg_grad, weight_term = dense_call(sums[0], *arrived, weight, grad_out)

    with jax.named_scope("gather_messages"):
        group = jnp.stack([msg_grad] + [col_permute(msg_grad, zl=k) for k in (1, 2, 3)])
        groups = [group] + [col_permute(group, x=k) for k in (1, 2, 3)]

    with jax.named_scope("reduce_weight"):
        weight_grad = reduce_weight(weight_term) * (1.0 / math.sqrt(node_total))

    own, sent = tile_call(
        backward_kernel, "backward_tiles", count, col_ids, row_ids, groups, tiles, [(8, edge, width)] * 2
    )

    with jax.named_scope("reduce_features"):
        both = add_all([own, row_permute(sent, core=1)]).astype(BF16).reshape(4, 2, edge, width)
        quads = [both[0]] + [row_permute(both[k], y=k) for k in (1, 2, 3)]
        kept = add_all([quad[0] for quad in quads])
        given = add_all([quad[1] for quad in quads]).astype(BF16)
        x_grad = (kept + row_permute(given, zh=1).astype(F32)).astype(BF16)

    return (activation, weight_grad, x_grad)


def solution(mesh):
    return jax.shard_map(
        local,
        mesh=mesh,
        in_specs=(
            P(("col", "row"), None),
            P("row", "col", None, None, None),
            P("row", "col", None),
            P("row", "col", None),
            P("row", "col"),
            P(),
            P(("row", "col"), None),
        ),
        out_specs=(P(("row", "col"), None), P(), P(("col", "row"), None)),
        check_vma=False,
    )
```

time: 699 us -> 197 us (0.28)
  waiting for transfers between devices: 595 us -> 89.3 us
  starting transfers between devices: 0.2 us -> 75.6 us
  other arithmetic: 39.5 us -> 7.97 us
  local copies, waits for them, and re-layouts: 32.6 us -> 4.45 us
  Pallas kernels: 0 us -> 15.8 us
  matrix products: 13.7 us -> 0 us
  between operations: 14.5 us -> 1.58 us
    psum x1 -> x0, waiting for transfers between devices: 229 us -> none  [local(): weight_total = lax.psum(weight_term, ('row', 'col'))]
    reduce_scatter x2 -> x0, waiting for transfers between devices: 229 us -> none  [the longest x1 140 us: local(): lax.psum_scatter(partial_rows.astype(jnp.bfloat16), 'col', scatter_dimens...]
    all_gather x2 -> x0, waiting for transfers between devices: 137 us -> none  [the longest x1 68.7 us: local(): msg_block = lax.all_gather(msg_grad, 'col', axis=0, tiled=True)]
    ppermute x0 -> x38, waiting for transfers between devices: none -> 89.3 us  [the longest x18 52.2 us: col_permute(): return lax.ppermute(value, 'col', pairs)]
    ppermute x0 -> x38, starting transfers between devices: none -> 75.6 us  [the longest x20 40.3 us: row_permute(): return lax.ppermute(value, 'row', pairs)]
    scatter-add x6 -> x0, other arithmetic: 25.8 us -> none  [the longest x3 12.9 us: forward_group(): return running.at[group_rows].add(product * active[:, None, None])]
    pallas_call x0 -> x3, Pallas kernels: none -> 15.8 us  [the longest x2 13.4 us: tile_call(): pl.pallas_call(kernel, out_shape=[jax.ShapeDtypeStruct(shape, BF16) for s...]
    dot_general x9 -> x0, matrix products: 13.7 us -> none  [the longest x3 5.03 us: backward_group(): jnp.einsum('gij,gif->gjf', block_tiles, msg_tiles[group_rows], preferred_...]
  transfers between devices with their start and end apart: 5 -> 38, of which waited for: 5 -> 22; matrix products, arithmetic and copies ran while one was open for 7% -> 3% of each run, Pallas kernels for 0% -> 3%
where the time goes in v1:
time: 197 us; the launch traced here: 195 us
  waiting for transfers between devices  89.3 us (45%)
  starting transfers between devices  75.6 us (38%)
  Pallas kernels  15.8 us (8%)
  other arithmetic  7.97 us (4%)
  local copies, waits for them, and re-layouts  4.45 us (2%)
    ppermute x18, waiting for transfers between devices, col_permute(): return lax.ppermute(value, 'col', pairs)  52.2 us
    ppermute x20, starting transfers between devices, row_permute(): return lax.ppermute(value, 'row', pairs)  40.3 us
    ppermute x20, waiting for transfers between devices, row_permute(): return lax.ppermute(value, 'row', pairs)  37.2 us
    ppermute x18, starting transfers between devices, col_permute(): return lax.ppermute(value, 'col', pairs)  35.3 us
    pallas_call x2, Pallas kernels, tile_call(): pl.pallas_call(kernel, out_shape=[jax.ShapeDtypeStruct(shape, BF16) for s...  13.4 us
  transfers between devices with their start and end apart: 38, of which 22 were waited for; matrix products, arithmetic and copies ran while one was open for 3% of the time, Pallas kernels for 3%

profile of v1, /device:TPU:2, one launch (start us, length us, event | category | flops | bytes accessed | tf_op | source)
XLA Modules:
  0.0 194.8 jit_solution(12892997636222060031)
XLA Ops:
  0.6 7.3 %collective-permute-start = (bf16[256,256]{1,0:T(8,128)(2,1)}, bf16[256,256]{1,0:T(8,128)(2,1)S(1)}, u32[]{:S(2)}, u32[]{:S(2)}) collective-permute-start(bf16[256,256]{1,0:T(8,128)(2,1)} %param.7), channel_id=1, source_target_pairs={{0,128},{16,144},{32,160},{48,176},{64,192},{80,208},{96,224},{112... | collective-permute-start | bytes 393224 | tf_op jit(solution)/shard_map/gather_features/ppermute | solution.py:24
  7.9 3.8 %collective-permute-done = bf16[256,256]{1,0:T(8,128)(2,1)S(1)} collective-permute-done((bf16[256,256]{1,0:T(8,128)(2,1)}, bf16[256,256]{1,0:T(8,128)(2,1)S(1)}, u32[]{:S(2)}, u32[]{:S(2)}) %collective-permute-start) | collective-permute-done | bytes 131104 | tf_op jit(solution)/shard_map/gather_features/ppermute | solution.py:24
  11.7 0.9 pad_maximum_fusion.1
  12.6 1.7 collective-permute-start.1
  14.3 0.9 constant_dynamic-update-slice_fusion.4
  15.2 1.7 collective-permute-start.3
  17.0 2.0 %collective-permute-start.2 = (bf16[2,256,256]{2,1,0:T(8,128)(2,1)S(1)}, bf16[2,256,256]{2,1,0:T(8,128)(2,1)S(1)}, u32[]{:S(2)}, u32[]{:S(2)}) collective-permute-start(bf16[2,256,256]{2,1,0:T(8,128)(2,1)S(1)} %pad_maximum_fusion.1), channel_id=1, source_target_pairs={{0,64},{16,80},{32,96},{48,112},{64,0},{80,16},{96,32},{112,48},{1... | collective-permute-start | bytes 786440 | tf_op jit(solution)/shard_map/gather_features/ppermute | solution.py:24
  19.0 3.1 %collective-permute-done.1 = bf16[2,256,256]{2,1,0:T(8,128)(2,1)S(1)} collective-permute-done((bf16[2,256,256]{2,1,0:T(8,128)(2,1)S(1)}, bf16[2,256,256]{2,1,0:T(8,128)(2,1)S(1)}, u32[]{:S(2)}, u32[]{:S(2)}) %collective-permute-start.1) | collective-permute-done | bytes 262176 | tf_op jit(solution)/shard_map/gather_features/ppermute | solution.py:24
  22.1 6.1 %collective-permute-done.2 = bf16[2,256,256]{2,1,0:T(8,128)(2,1)S(1)} collective-permute-done((bf16[2,256,256]{2,1,0:T(8,128)(2,1)S(1)}, bf16[2,256,256]{2,1,0:T(8,128)(2,1)S(1)}, u32[]{:S(2)}, u32[]{:S(2)}) %collective-permute-start.2) | collective-permute-done | bytes 262176 | tf_op jit(solution)/shard_map/gather_features/ppermute | solution.py:24
  29.0 2.0 %collective-permute-done.4.far = bf16[8,256,256]{2,1,0:T(8,128)(2,1)S(1)} collective-permute-done((bf16[8,256,256]{2,1,0:T(8,128)(2,1)S(1)}, bf16[8,256,256]{2,1,0:T(8,128)(2,1)S(1)}, u32[]{:S(2)}, u32[]{:S(2)}) %collective-permute-start.4) | collective-permute-done | bytes 1048608 | tf_op jit(solution)/shard_map/gather_features/ppermute | solution.py:24
  31.0 1.0 copy-done.2
  32.0 6.7 %forward_tiles.1 = (bf16[4,256,256]{2,1,0:T(8,128)(2,1)}, bf16[4,256,256]{2,1,0:T(8,128)(2,1)}, bf16[4,256,256]{2,1,0:T(8,128)(2,1)}, bf16[4,256,256]{2,1,0:T(8,128)(2,1)}) custom-call(s32[1]{0:T(128)} %bitcast.47.cnt, s32[80]{0:T(128)} %bitcast.76, s32[80]{0:T(128)} %bitcast.78, bf16[8,256,256]{2,1,0:T(8,128)(2,1)} %copy-done.1, ...), custom_call_target="tpu_custom_call" | custom-call | flops 2684354560 | bytes 10485760 | tf_op jit(solution)/shard_map/forward_tiles/pallas_call | solution.py:122
  38.6 0.3 collective-permute-start.5
  39.0 3.3 %collective-permute-start.6 = (bf16[4,256,256]{2,1,0:T(8,128)(2,1)}, bf16[4,256,256]{2,1,0:T(8,128)(2,1)S(1)}, u32[]{:S(2)}, u32[]{:S(2)}) collective-permute-start(bf16[4,256,256]{2,1,0:T(8,128)(2,1)} %get-tuple-element.14), channel_id=1, source_target_pairs={{0,8},{1,9},{2,10},{3,11},{4,12},{5,13},{6,14},{7,15},{8,0},{9,1},... | collective-permute-start | bytes 1572872 | tf_op jit(solution)/shard_map/reduce_aggregate/ppermute | solution.py:31
  42.3 1.2 collective-permute-start.7
  43.5 6.6 %collective-permute-done.5 = bf16[4,256,256]{2,1,0:T(8,128)(2,1)S(1)} collective-permute-done((bf16[4,256,256]{2,1,0:T(8,128)(2,1)}, bf16[4,256,256]{2,1,0:T(8,128)(2,1)S(1)}, u32[]{:S(2)}, u32[]{:S(2)}) %collective-permute-start.5) | collective-permute-done | bytes 524320 | tf_op jit(solution)/shard_map/reduce_aggregate/ppermute | solution.py:31
  50.1 1.4 collective-permute-done.6
  51.5 15.1 %collective-permute-done.7 = bf16[4,256,256]{2,1,0:T(8,128)(2,1)S(1)} collective-permute-done((bf16[4,256,256]{2,1,0:T(8,128)(2,1)}, bf16[4,256,256]{2,1,0:T(8,128)(2,1)S(1)}, u32[]{:S(2)}, u32[]{:S(2)}) %collective-permute-start.7) | collective-permute-done | bytes 524320 | tf_op jit(solution)/shard_map/reduce_aggregate/ppermute | solution.py:31
  66.6 2.0 %fusion.4 = (bf16[256,256]{1,0:T(8,128)(2,1)S(1)}, bf16[256,256]{1,0:T(8,128)(2,1)S(1)}, bf16[256,256]{1,0:T(8,128)(2,1)S(1)}, f32[256,256]{1,0:T(8,128)}) fusion(bf16[4,256,256]{2,1,0:T(8,128)(2,1)S(1)} %collective-permute-done.7, bf16[4,256,256]{2,1,0:T(8,128)(2,1)S(1)} %collective-permute-done.6, bf16[4,256,256]{2,1,0:T(8,128)(2,1)S(1)} %collective-permute-done.5, ...), kind=kLoop, calls=%fused_computation.14 | loop fusion | flops 2031616 | bytes 2752512 | tf_op jit(solution)/shard_map/reduce_aggregate/add | solution.py:212
  68.7 1.4 collective-permute-start.10
  70.1 4.6 %collective-permute-start.9 = (bf16[256,256]{1,0:T(8,128)(2,1)S(1)}, bf16[256,256]{1,0:T(8,128)(2,1)S(1)}, u32[]{:S(2)}, u32[]{:S(2)}) collective-permute-start(bf16[256,256]{1,0:T(8,128)(2,1)S(1)} %get-tuple-element.22), channel_id=1, source_target_pairs={{0,2},{1,3},{2,0},{3,1},{4,6},{5,7},{6,4},{7,5},{8,10},{9,11},{10,... | collective-permute-start | bytes 393224 | tf_op jit(solution)/shard_map/reduce_aggregate/ppermute | solution.py:31
  74.7 2.0 %collective-permute-start.8 = (bf16[256,256]{1,0:T(8,128)(2,1)S(1)}, bf16[256,256]{1,0:T(8,128)(2,1)S(1)}, u32[]{:S(2)}, u32[]{:S(2)}) collective-permute-start(bf16[256,256]{1,0:T(8,128)(2,1)S(1)} %get-tuple-element.23), channel_id=1, source_target_pairs={{0,1},{1,2},{2,3},{3,0},{4,5},{5,6},{6,7},{7,4},{8,9},{9,10},{10,1... | collective-permute-start | bytes 393224 | tf_op jit(solution)/shard_map/reduce_aggregate/ppermute | solution.py:31
  76.8 10.1 %collective-permute-done.9.q2 = bf16[256,256]{1,0:T(8,128)(2,1)S(1)} collective-permute-done((bf16[256,256]{1,0:T(8,128)(2,1)S(1)}, bf16[256,256]{1,0:T(8,128)(2,1)S(1)}, u32[]{:S(2)}, u32[]{:S(2)}) %collective-permute-start.9) | collective-permute-done | bytes 131104 | tf_op jit(solution)/shard_map/reduce_aggregate/ppermute | solution.py:31
  86.8 0.6 copy-done.7
  87.5 2.4 %dense.1 = (bf16[256,256]{1,0:T(8,128)(2,1)}, bf16[256,256]{1,0:T(8,128)(2,1)}, f32[256,256]{1,0:T(8,128)}) custom-call(f32[256,256]{1,0:T(8,128)} %get-tuple-element.24.own, bf16[256,256]{1,0:T(8,128)(2,1)} %copy-done.8, bf16[256,256]{1,0:T(8,128)(2,1)} %copy-done.7, bf16[256,256]{1,0:T(8,128)(2,1)} %copy-done.6, bf16[256,256]{1,0:T(8,128)(2,1)} %weight.1, ...), custom_call_target="tpu_custom_call" | custom-call | flops 100663296 | bytes 1000000 | tf_op jit(solution)/shard_map/dense/pallas_call | solution.py:160
  90.0 2.0 %collective-permute-start.27 = (bf16[256,256]{1,0:T(8,128)(2,1)}, bf16[256,256]{1,0:T(8,128)(2,1)S(1)}, u32[]{:S(2)}, u32[]{:S(2)}) collective-permute-start(bf16[256,256]{1,0:T(8,128)(2,1)} %get-tuple-element.18), channel_id=1, source_target_pairs={{0,1},{1,2},{2,3},{3,0},{4,5},{5,6},{6,7},{7,4},{8,9},{9,10},{10,1... | collective-permute-start | bytes 393224 | tf_op jit(solution)/shard_map/gather_messages/ppermute | solution.py:31
  92.0 0.9 constant_dynamic-slice_fusion.8
  93.0 3.3 %collective-permute-done.29 = bf16[256,256]{1,0:T(8,128)(2,1)S(1)} collective-permute-done((bf16[256,256]{1,0:T(8,128)(2,1)}, bf16[256,256]{1,0:T(8,128)(2,1)S(1)}, u32[]{:S(2)}, u32[]{:S(2)}) %collective-permute-start.29) | collective-permute-done | bytes 131104 | tf_op jit(solution)/shard_map/gather_messages/ppermute | solution.py:31
  96.3 5.7 %collective-permute-done.28 = bf16[256,256]{1,0:T(8,128)(2,1)S(1)} collective-permute-done((bf16[256,256]{1,0:T(8,128)(2,1)}, bf16[256,256]{1,0:T(8,128)(2,1)S(1)}, u32[]{:S(2)}, u32[]{:S(2)}) %collective-permute-start.28) | collective-permute-done | bytes 131104 | tf_op jit(solution)/shard_map/gather_messages/ppermute | solution.py:31
  102.1 1.0 pad_maximum_fusion.g0
  103.1 0.3 collective-permute-start.32
  103.3 3.3 %collective-permute-start.31 = (bf16[4,256,256]{2,1,0:T(8,128)(2,1)S(1)}, bf16[4,256,256]{2,1,0:T(8,128)(2,1)S(1)}, u32[]{:S(2)}, u32[]{:S(2)}) collective-permute-start(bf16[4,256,256]{2,1,0:T(8,128)(2,1)S(1)} %pad_maximum_fusion.g0), channel_id=1, source_target_pairs={{0,8},{1,9},{2,10},{3,11},{4,12},{5,13},{6,14},{7,15},{8,0},{9,1},... | collective-permute-start | bytes 1572872 | tf_op jit(solution)/shard_map/gather_messages/ppermute | solution.py:31
  106.7 2.5 %collective-permute-start.30 = (bf16[4,256,256]{2,1,0:T(8,128)(2,1)S(1)}, bf16[4,256,256]{2,1,0:T(8,128)(2,1)S(1)}, u32[]{:S(2)}, u32[]{:S(2)}) collective-permute-start(bf16[4,256,256]{2,1,0:T(8,128)(2,1)S(1)} %pad_maximum_fusion.g0), channel_id=1, source_target_pairs={{0,4},{1,5},{2,6},{3,7},{4,8},{5,9},{6,10},{7,11},{8,12},{9,13},{1... | collective-permute-start | bytes 1572872 | tf_op jit(solution)/shard_map/gather_messages/ppermute | solution.py:31
  109.2 0.9 dynamic-slice_add_fusion
  110.1 0.8 collective-permute-start.12
  110.9 2.6 %collective-permute-start.14 = (f32[32,256]{1,0:T(8,128)S(1)}, f32[32,256]{1,0:T(8,128)S(1)}, u32[]{:S(2)}, u32[]{:S(2)}) collective-permute-start(f32[32,256]{1,0:T(8,128)S(1)} %get-tuple-element.33), channel_id=1, source_target_pairs={{0,96},{16,112},{32,0},{48,16},{64,32},{80,48},{96,64},{112,80},{1... | collective-permute-start | bytes 98312 | tf_op jit(solution)/shard_map/reduce_weight/ppermute | solution.py:24
  113.5 1.9 collective-permute-done.12
  115.4 5.4 %collective-permute-done.13 = f32[32,256]{1,0:T(8,128)S(1)} collective-permute-done((f32[32,256]{1,0:T(8,128)S(1)}, f32[32,256]{1,0:T(8,128)S(1)}, u32[]{:S(2)}, u32[]{:S(2)}) %collective-permute-start.13) | collective-permute-done | bytes 32800 | tf_op jit(solution)/shard_map/reduce_weight/ppermute | solution.py:24
  120.8 6.6 %collective-permute-start.15 = (f32[16,256]{1,0:T(8,128)S(1)}, f32[16,256]{1,0:T(8,128)S(1)}, u32[]{:S(2)}, u32[]{:S(2)}) collective-permute-start(f32[16,256]{1,0:T(8,128)S(1)} %constant_dynamic-slice_fusion.4), channel_id=1, source_target_pairs={{0,128},{16,144},{32,160},{48,176},{64,192},{80,208},{96,224},{112... | collective-permute-start | bytes 49160 | tf_op jit(solution)/shard_map/reduce_weight/ppermute | solution.py:24
  127.4 1.7 collective-permute-done.31.g2
  129.1 0.9 collective-permute-done.30.g1
  130.0 0.8 copy-done.5
  130.8 6.8 %backward_tiles.1 = (bf16[8,256,256]{2,1,0:T(8,128)(2,1)}, bf16[8,256,256]{2,1,0:T(8,128)(2,1)}) custom-call(s32[1]{0:T(128)} %bitcast.48.cnt, s32[80]{0:T(128)} %bitcast.79, s32[80]{0:T(128)} %bitcast.77, bf16[4,256,256]{2,1,0:T(8,128)(2,1)} %copy-done, bf16[4,256,256]{2,1,0:T(8,128)(2,1)} %copy-done.5, bf16[4,256,256]{2,1,0:T(8,128)(2,1)} %copy-done.4, ...), custom_call_target="tpu_custom_call" | custom-call | flops 2684354560 | bytes 10485760 | tf_op jit(solution)/shard_map/backward_tiles/pallas_call | solution.py:122
  137.7 8.4 %collective-permute-start.18 = (f32[16,256]{1,0:T(8,128)S(1)}, f32[16,256]{1,0:T(8,128)S(1)}, u32[]{:S(2)}, u32[]{:S(2)}) collective-permute-start(f32[16,256]{1,0:T(8,128)S(1)} %dynamic-slice_add_fusion.3), channel_id=1, source_target_pairs={{0,12},{1,13},{2,14},{3,15},{4,0},{5,1},{6,2},{7,3},{8,4},{9,5},{1... | collective-permute-start | bytes 49160 | tf_op jit(solution)/shard_map/reduce_weight/ppermute | solution.py:31
  146.1 1.6 collective-permute-start.16
  147.7 3.7 %collective-permute-done.17 = f32[16,256]{1,0:T(8,128)S(1)} collective-permute-done((f32[16,256]{1,0:T(8,128)S(1)}, f32[16,256]{1,0:T(8,128)S(1)}, u32[]{:S(2)}, u32[]{:S(2)}) %collective-permute-start.17) | collective-permute-done | bytes 16416 | tf_op jit(solution)/shard_map/reduce_weight/ppermute | solution.py:31
  151.4 2.1 %collective-permute-start.21 = (f32[16,256]{1,0:T(8,128)S(1)}, f32[16,256]{1,0:T(8,128)S(1)}, u32[]{:S(2)}, u32[]{:S(2)}) collective-permute-start(f32[16,256]{1,0:T(8,128)S(1)} %fusion.8), channel_id=1, source_target_pairs={{0,3},{1,0},{2,1},{3,2},{4,7},{5,4},{6,5},{7,6},{8,11},{9,8},{10,9... | collective-permute-start | bytes 49160 | tf_op jit(solution)/shard_map/reduce_weight/ppermute | solution.py:31
  153.7 1.9 collective-permute-start.19
  155.6 2.6 %collective-permute-done.20 = f32[16,256]{1,0:T(8,128)S(1)} collective-permute-done((f32[16,256]{1,0:T(8,128)S(1)}, f32[16,256]{1,0:T(8,128)S(1)}, u32[]{:S(2)}, u32[]{:S(2)}) %collective-permute-start.20) | collective-permute-done | bytes 16416 | tf_op jit(solution)/shard_map/reduce_weight/ppermute | solution.py:31
  158.2 1.0 collective-permute-done.19
  159.2 3.3 %collective-permute-start.22 = (f32[16,256]{1,0:T(8,128)S(1)}, f32[16,256]{1,0:T(8,128)S(1)}, u32[]{:S(2)}, u32[]{:S(2)}) collective-permute-start(f32[16,256]{1,0:T(8,128)S(1)} %fusion.7), channel_id=1, source_target_pairs={{0,128},{16,144},{32,160},{48,176},{64,192},{80,208},{96,224},{112... | collective-permute-start | bytes 49160 | tf_op jit(solution)/shard_map/reduce_weight/ppermute | solution.py:24
  162.5 4.4 %collective-permute-done.22 = f32[16,256]{1,0:T(8,128)S(1)} collective-permute-done((f32[16,256]{1,0:T(8,128)S(1)}, f32[16,256]{1,0:T(8,128)S(1)}, u32[]{:S(2)}, u32[]{:S(2)}) %collective-permute-start.22) | collective-permute-done | bytes 16416 | tf_op jit(solution)/shard_map/reduce_weight/ppermute | solution.py:24
  167.0 1.0 collective-permute-start.25
  168.0 2.5 %collective-permute-start.24 = (f32[32,256]{1,0:T(8,128)S(1)}, f32[32,256]{1,0:T(8,128)S(1)}, u32[]{:S(2)}, u32[]{:S(2)}) collective-permute-start(f32[32,256]{1,0:T(8,128)S(1)} %bitcast.58), channel_id=1, source_target_pairs={{0,64},{16,80},{32,96},{48,112},{64,0},{80,16},{96,32},{112,48},{1... | collective-permute-start | bytes 98312 | tf_op jit(solution)/shard_map/reduce_weight/ppermute | solution.py:24
  170.5 1.3 collective-permute-start.23
  171.8 1.5 add_convert_fusion
  173.5 3.2 %collective-permute-start.36 = (bf16[2,256,256]{2,1,0:T(8,128)(2,1)S(1)}, bf16[2,256,256]{2,1,0:T(8,128)(2,1)S(1)}, u32[]{:S(2)}, u32[]{:S(2)}) collective-permute-start(bf16[2,256,256]{2,1,0:T(8,128)(2,1)S(1)} %get-tuple-element.26), channel_id=1, source_target_pairs={{0,96},{16,112},{32,0},{48,16},{64,32},{80,48},{96,64},{112,80},{1... | collective-permute-start | bytes 786440 | tf_op jit(solution)/shard_map/reduce_features/ppermute | solution.py:24
  177.0 5.2 %collective-permute-done.34 = bf16[2,256,256]{2,1,0:T(8,128)(2,1)S(1)} collective-permute-done((bf16[2,256,256]{2,1,0:T(8,128)(2,1)S(1)}, bf16[2,256,256]{2,1,0:T(8,128)(2,1)S(1)}, u32[]{:S(2)}, u32[]{:S(2)}) %collective-permute-start.34) | collective-permute-done | bytes 262176 | tf_op jit(solution)/shard_map/reduce_features/ppermute | solution.py:24
  182.2 1.4 collective-permute-done.36
  183.6 1.4 collective-permute-done.35
  185.1 5.8 %collective-permute-start.37 = (bf16[256,256]{1,0:T(8,128)(2,1)S(1)}, bf16[256,256]{1,0:T(8,128)(2,1)S(1)}, u32[]{:S(2)}, u32[]{:S(2)}) collective-permute-start(bf16[256,256]{1,0:T(8,128)(2,1)S(1)} %fusion.5), channel_id=1, source_target_pairs={{0,128},{16,144},{32,160},{48,176},{64,192},{80,208},{96,224},{112... | collective-permute-start | bytes 393224 | tf_op jit(solution)/shard_map/reduce_features/ppermute | solution.py:24
  190.9 0.7 fusion
  191.6 2.4 %collective-permute-done.37 = bf16[256,256]{1,0:T(8,128)(2,1)S(1)} collective-permute-done((bf16[256,256]{1,0:T(8,128)(2,1)S(1)}, bf16[256,256]{1,0:T(8,128)(2,1)S(1)}, u32[]{:S(2)}, u32[]{:S(2)}) %collective-permute-start.37) | collective-permute-done | bytes 131104 | tf_op jit(solution)/shard_map/reduce_features/ppermute | solution.py:24
  194.0 0.7 fusion.1
  (62 shorter events, 1.2 us)
Async XLA Ops:
  0.6 11.1 %collective-permute-start = (bf16[256,256]{1,0:T(8,128)(2,1)}, bf16[256,256]{1,0:T(8,128)(2,1)S(1)}, u32[]{:S(2)}, u32[]{:S(2)}) collective-permute-start(bf16[256,256]{1,0:T(8,128)(2,1)} %param.7), channel_id=1, source_target_pairs={{0,128},{16,144},{32,160},{48,176},{64,192},{80,208},{96,224},{112... | collective-permute-start | bytes 393224 | tf_op jit(solution)/shard_map/gather_features/ppermute | solution.py:24
  12.6 9.4 %collective-permute-start.1 = (bf16[2,256,256]{2,1,0:T(8,128)(2,1)S(1)}, bf16[2,256,256]{2,1,0:T(8,128)(2,1)S(1)}, u32[]{:S(2)}, u32[]{:S(2)}) collective-permute-start(bf16[2,256,256]{2,1,0:T(8,128)(2,1)S(1)} %pad_maximum_fusion.1), channel_id=1, source_target_pairs={{0,32},{16,48},{32,64},{48,80},{64,96},{80,112},{96,0},{112,16},{1... | collective-permute-start | bytes 786440 | tf_op jit(solution)/shard_map/gather_features/ppermute | solution.py:24
  15.2 13.0 %collective-permute-start.3 = (bf16[2,256,256]{2,1,0:T(8,128)(2,1)S(1)}, bf16[2,256,256]{2,1,0:T(8,128)(2,1)S(1)}, u32[]{:S(2)}, u32[]{:S(2)}) collective-permute-start(bf16[2,256,256]{2,1,0:T(8,128)(2,1)S(1)} %pad_maximum_fusion.1), channel_id=1, source_target_pairs={{0,96},{16,112},{32,0},{48,16},{64,32},{80,48},{96,64},{112,80},{1... | collective-permute-start | bytes 786440 | tf_op jit(solution)/shard_map/gather_features/ppermute | solution.py:24
  17.0 11.2 %collective-permute-start.2 = (bf16[2,256,256]{2,1,0:T(8,128)(2,1)S(1)}, bf16[2,256,256]{2,1,0:T(8,128)(2,1)S(1)}, u32[]{:S(2)}, u32[]{:S(2)}) collective-permute-start(bf16[2,256,256]{2,1,0:T(8,128)(2,1)S(1)} %pad_maximum_fusion.1), channel_id=1, source_target_pairs={{0,64},{16,80},{32,96},{48,112},{64,0},{80,16},{96,32},{112,48},{1... | collective-permute-start | bytes 786440 | tf_op jit(solution)/shard_map/gather_features/ppermute | solution.py:24
  28.2 2.8 %copy-start.1 = (bf16[8,256,256]{2,1,0:T(8,128)(2,1)}, bf16[8,256,256]{2,1,0:T(8,128)(2,1)S(1)}, u32[]{:S(2)}) copy-start(bf16[8,256,256]{2,1,0:T(8,128)(2,1)S(1)} %constant_dynamic-update-slice_fusion.near) | copy-start | bytes 3145732
  28.3 2.7 %collective-permute-start.4 = (bf16[8,256,256]{2,1,0:T(8,128)(2,1)S(1)}, bf16[8,256,256]{2,1,0:T(8,128)(2,1)S(1)}, u32[]{:S(2)}, u32[]{:S(2)}) collective-permute-start(bf16[8,256,256]{2,1,0:T(8,128)(2,1)S(1)} %constant_dynamic-update-slice_fusion.near), channel_id=1, source_target_pairs={{0,16},{16,0},{32,48},{48,32},{64,80},{80,64},{96,112},{112,96},{1... | collective-permute-start | bytes 3145736 | tf_op jit(solution)/shard_map/gather_features/ppermute | solution.py:24
  31.0 1.0 copy-start.2
  38.6 11.4 %collective-permute-start.5 = (bf16[4,256,256]{2,1,0:T(8,128)(2,1)}, bf16[4,256,256]{2,1,0:T(8,128)(2,1)S(1)}, u32[]{:S(2)}, u32[]{:S(2)}) collective-permute-start(bf16[4,256,256]{2,1,0:T(8,128)(2,1)} %get-tuple-element.13), channel_id=1, source_target_pairs={{0,4},{1,5},{2,6},{3,7},{4,8},{5,9},{6,10},{7,11},{8,12},{9,13},{1... | collective-permute-start | bytes 1572872 | tf_op jit(solution)/shard_map/reduce_aggregate/ppermute | solution.py:31
  39.0 12.5 %collective-permute-start.6 = (bf16[4,256,256]{2,1,0:T(8,128)(2,1)}, bf16[4,256,256]{2,1,0:T(8,128)(2,1)S(1)}, u32[]{:S(2)}, u32[]{:S(2)}) collective-permute-start(bf16[4,256,256]{2,1,0:T(8,128)(2,1)} %get-tuple-element.14), channel_id=1, source_target_pairs={{0,8},{1,9},{2,10},{3,11},{4,12},{5,13},{6,14},{7,15},{8,0},{9,1},... | collective-permute-start | bytes 1572872 | tf_op jit(solution)/shard_map/reduce_aggregate/ppermute | solution.py:31
  42.3 24.3 %collective-permute-start.7 = (bf16[4,256,256]{2,1,0:T(8,128)(2,1)}, bf16[4,256,256]{2,1,0:T(8,128)(2,1)S(1)}, u32[]{:S(2)}, u32[]{:S(2)}) collective-permute-start(bf16[4,256,256]{2,1,0:T(8,128)(2,1)} %get-tuple-element.15), channel_id=1, source_target_pairs={{0,12},{1,13},{2,14},{3,15},{4,0},{5,1},{6,2},{7,3},{8,4},{9,5},{1... | collective-permute-start | bytes 1572872 | tf_op jit(solution)/shard_map/reduce_aggregate/ppermute | solution.py:31
  68.7 8.1 %collective-permute-start.10 = (bf16[256,256]{1,0:T(8,128)(2,1)S(1)}, bf16[256,256]{1,0:T(8,128)(2,1)S(1)}, u32[]{:S(2)}, u32[]{:S(2)}) collective-permute-start(bf16[256,256]{1,0:T(8,128)(2,1)S(1)} %get-tuple-element.21), channel_id=1, source_target_pairs={{0,3},{1,0},{2,1},{3,2},{4,7},{5,4},{6,5},{7,6},{8,11},{9,8},{10,9... | collective-permute-start | bytes 393224 | tf_op jit(solution)/shard_map/reduce_aggregate/ppermute | solution.py:31
  70.1 16.7 %collective-permute-start.9 = (bf16[256,256]{1,0:T(8,128)(2,1)S(1)}, bf16[256,256]{1,0:T(8,128)(2,1)S(1)}, u32[]{:S(2)}, u32[]{:S(2)}) collective-permute-start(bf16[256,256]{1,0:T(8,128)(2,1)S(1)} %get-tuple-element.22), channel_id=1, source_target_pairs={{0,2},{1,3},{2,0},{3,1},{4,6},{5,7},{6,4},{7,5},{8,10},{9,11},{10,... | collective-permute-start | bytes 393224 | tf_op jit(solution)/shard_map/reduce_aggregate/ppermute | solution.py:31
  74.7 12.1 %collective-permute-start.8 = (bf16[256,256]{1,0:T(8,128)(2,1)S(1)}, bf16[256,256]{1,0:T(8,128)(2,1)S(1)}, u32[]{:S(2)}, u32[]{:S(2)}) collective-permute-start(bf16[256,256]{1,0:T(8,128)(2,1)S(1)} %get-tuple-element.23), channel_id=1, source_target_pairs={{0,1},{1,2},{2,3},{3,0},{4,5},{5,6},{6,7},{7,4},{8,9},{9,10},{10,1... | collective-permute-start | bytes 393224 | tf_op jit(solution)/shard_map/reduce_aggregate/ppermute | solution.py:31
  76.8 10.1 %copy-start.6 = (bf16[256,256]{1,0:T(8,128)(2,1)}, bf16[256,256]{1,0:T(8,128)(2,1)S(1)}, u32[]{:S(2)}) copy-start(bf16[256,256]{1,0:T(8,128)(2,1)S(1)} %collective-permute-done.10.q3) | copy-start | bytes 393220
  86.8 0.6 copy-start.7
  86.8 0.7 copy-start.8
  90.0 6.4 %collective-permute-start.29 = (bf16[256,256]{1,0:T(8,128)(2,1)}, bf16[256,256]{1,0:T(8,128)(2,1)S(1)}, u32[]{:S(2)}, u32[]{:S(2)}) collective-permute-start(bf16[256,256]{1,0:T(8,128)(2,1)} %get-tuple-element.18), channel_id=1, source_target_pairs={{0,3},{1,0},{2,1},{3,2},{4,7},{5,4},{6,5},{7,6},{8,11},{9,8},{10,9... | collective-permute-start | bytes 393224 | tf_op jit(solution)/shard_map/gather_messages/ppermute | solution.py:31
  90.0 12.1 %collective-permute-start.28 = (bf16[256,256]{1,0:T(8,128)(2,1)}, bf16[256,256]{1,0:T(8,128)(2,1)S(1)}, u32[]{:S(2)}, u32[]{:S(2)}) collective-permute-start(bf16[256,256]{1,0:T(8,128)(2,1)} %get-tuple-element.18), channel_id=1, source_target_pairs={{0,2},{1,3},{2,0},{3,1},{4,6},{5,7},{6,4},{7,5},{8,10},{9,11},{10,... | collective-permute-start | bytes 393224 | tf_op jit(solution)/shard_map/gather_messages/ppermute | solution.py:31
  90.0 12.1 %collective-permute-start.27 = (bf16[256,256]{1,0:T(8,128)(2,1)}, bf16[256,256]{1,0:T(8,128)(2,1)S(1)}, u32[]{:S(2)}, u32[]{:S(2)}) collective-permute-start(bf16[256,256]{1,0:T(8,128)(2,1)} %get-tuple-element.18), channel_id=1, source_target_pairs={{0,1},{1,2},{2,3},{3,0},{4,5},{5,6},{6,7},{7,4},{8,9},{9,10},{10,1... | collective-permute-start | bytes 393224 | tf_op jit(solution)/shard_map/gather_messages/ppermute | solution.py:31
  92.9 16.3 %collective-permute-start.11 = (f32[128,256]{1,0:T(8,128)S(1)}, f32[128,256]{1,0:T(8,128)S(1)}, u32[]{:S(2)}, u32[]{:S(2)}) collective-permute-start(f32[128,256]{1,0:T(8,128)S(1)} %constant_dynamic-slice_fusion.8), channel_id=1, source_target_pairs={{0,16},{16,0},{32,48},{48,32},{64,80},{80,64},{96,112},{112,96},{1... | collective-permute-start | bytes 393224 | tf_op jit(solution)/shard_map/reduce_weight/ppermute | solution.py:24
  103.0 26.9 %copy-start = (bf16[4,256,256]{2,1,0:T(8,128)(2,1)}, bf16[4,256,256]{2,1,0:T(8,128)(2,1)S(1)}, u32[]{:S(2)}) copy-start(bf16[4,256,256]{2,1,0:T(8,128)(2,1)S(1)} %pad_maximum_fusion.g0) | copy-start | bytes 1572868
  103.1 24.3 %collective-permute-start.32 = (bf16[4,256,256]{2,1,0:T(8,128)(2,1)S(1)}, bf16[4,256,256]{2,1,0:T(8,128)(2,1)S(1)}, u32[]{:S(2)}, u32[]{:S(2)}) collective-permute-start(bf16[4,256,256]{2,1,0:T(8,128)(2,1)S(1)} %pad_maximum_fusion.g0), channel_id=1, source_target_pairs={{0,12},{1,13},{2,14},{3,15},{4,0},{5,1},{6,2},{7,3},{8,4},{9,5},{1... | collective-permute-start | bytes 1572872 | tf_op jit(solution)/shard_map/gather_messages/ppermute | solution.py:31
  103.3 25.7 %collective-permute-start.31 = (bf16[4,256,256]{2,1,0:T(8,128)(2,1)S(1)}, bf16[4,256,256]{2,1,0:T(8,128)(2,1)S(1)}, u32[]{:S(2)}, u32[]{:S(2)}) collective-permute-start(bf16[4,256,256]{2,1,0:T(8,128)(2,1)S(1)} %pad_maximum_fusion.g0), channel_id=1, source_target_pairs={{0,8},{1,9},{2,10},{3,11},{4,12},{5,13},{6,14},{7,15},{8,0},{9,1},... | collective-permute-start | bytes 1572872 | tf_op jit(solution)/shard_map/gather_messages/ppermute | solution.py:31
  106.7 23.3 %collective-permute-start.30 = (bf16[4,256,256]{2,1,0:T(8,128)(2,1)S(1)}, bf16[4,256,256]{2,1,0:T(8,128)(2,1)S(1)}, u32[]{:S(2)}, u32[]{:S(2)}) collective-permute-start(bf16[4,256,256]{2,1,0:T(8,128)(2,1)S(1)} %pad_maximum_fusion.g0), channel_id=1, source_target_pairs={{0,4},{1,5},{2,6},{3,7},{4,8},{5,9},{6,10},{7,11},{8,12},{9,13},{1... | collective-permute-start | bytes 1572872 | tf_op jit(solution)/shard_map/gather_messages/ppermute | solution.py:31
  110.1 5.2 %collective-permute-start.12 = (f32[32,256]{1,0:T(8,128)S(1)}, f32[32,256]{1,0:T(8,128)S(1)}, u32[]{:S(2)}, u32[]{:S(2)}) collective-permute-start(f32[32,256]{1,0:T(8,128)S(1)} %get-tuple-element.32), channel_id=1, source_target_pairs={{0,32},{16,48},{32,64},{48,80},{64,96},{80,112},{96,0},{112,16},{1... | collective-permute-start | bytes 98312 | tf_op jit(solution)/shard_map/reduce_weight/ppermute | solution.py:24
  110.9 4.4 %collective-permute-start.14 = (f32[32,256]{1,0:T(8,128)S(1)}, f32[32,256]{1,0:T(8,128)S(1)}, u32[]{:S(2)}, u32[]{:S(2)}) collective-permute-start(f32[32,256]{1,0:T(8,128)S(1)} %get-tuple-element.33), channel_id=1, source_target_pairs={{0,96},{16,112},{32,0},{48,16},{64,32},{80,48},{96,64},{112,80},{1... | collective-permute-start | bytes 98312 | tf_op jit(solution)/shard_map/reduce_weight/ppermute | solution.py:24
  115.3 5.4 %collective-permute-start.13 = (f32[32,256]{1,0:T(8,128)S(1)}, f32[32,256]{1,0:T(8,128)S(1)}, u32[]{:S(2)}, u32[]{:S(2)}) collective-permute-start(f32[32,256]{1,0:T(8,128)S(1)} %get-tuple-element.34), channel_id=1, source_target_pairs={{0,64},{16,80},{32,96},{48,112},{64,0},{80,16},{96,32},{112,48},{1... | collective-permute-start | bytes 98312 | tf_op jit(solution)/shard_map/reduce_weight/ppermute | solution.py:24
  120.8 16.8 %collective-permute-start.15 = (f32[16,256]{1,0:T(8,128)S(1)}, f32[16,256]{1,0:T(8,128)S(1)}, u32[]{:S(2)}, u32[]{:S(2)}) collective-permute-start(f32[16,256]{1,0:T(8,128)S(1)} %constant_dynamic-slice_fusion.4), channel_id=1, source_target_pairs={{0,128},{16,144},{32,160},{48,176},{64,192},{80,208},{96,224},{112... | collective-permute-start | bytes 49160 | tf_op jit(solution)/shard_map/reduce_weight/ppermute | solution.py:24
  127.4 2.6 %copy-start.3 = (bf16[4,256,256]{2,1,0:T(8,128)(2,1)}, bf16[4,256,256]{2,1,0:T(8,128)(2,1)S(1)}, u32[]{:S(2)}) copy-start(bf16[4,256,256]{2,1,0:T(8,128)(2,1)S(1)} %collective-permute-done.32.g3) | copy-start | bytes 1572868
  129.1 0.9 copy-start.4
  130.0 0.8 copy-start.5
  137.5 34.3 %collective-permute-start.33 = (bf16[8,256,256]{2,1,0:T(8,128)(2,1)}, bf16[8,256,256]{2,1,0:T(8,128)(2,1)S(1)}, u32[]{:S(2)}, u32[]{:S(2)}) collective-permute-start(bf16[8,256,256]{2,1,0:T(8,128)(2,1)} %get-tuple-element.20), channel_id=1, source_target_pairs={{0,16},{16,0},{32,48},{48,32},{64,80},{80,64},{96,112},{112,96},{1... | collective-permute-start | bytes 3145736 | tf_op jit(solution)/shard_map/reduce_features/ppermute | solution.py:24
  137.7 10.0 %collective-permute-start.18 = (f32[16,256]{1,0:T(8,128)S(1)}, f32[16,256]{1,0:T(8,128)S(1)}, u32[]{:S(2)}, u32[]{:S(2)}) collective-permute-start(f32[16,256]{1,0:T(8,128)S(1)} %dynamic-slice_add_fusion.3), channel_id=1, source_target_pairs={{0,12},{1,13},{2,14},{3,15},{4,0},{5,1},{6,2},{7,3},{8,4},{9,5},{1... | collective-permute-start | bytes 49160 | tf_op jit(solution)/shard_map/reduce_weight/ppermute | solution.py:31
  146.1 5.2 %collective-permute-start.17 = (f32[16,256]{1,0:T(8,128)S(1)}, f32[16,256]{1,0:T(8,128)S(1)}, u32[]{:S(2)}, u32[]{:S(2)}) collective-permute-start(f32[16,256]{1,0:T(8,128)S(1)} %dynamic-slice_add_fusion.3), channel_id=1, source_target_pairs={{0,8},{1,9},{2,10},{3,11},{4,12},{5,13},{6,14},{7,15},{8,0},{9,1},... | collective-permute-start | bytes 49160 | tf_op jit(solution)/shard_map/reduce_weight/ppermute | solution.py:31
  146.1 5.2 %collective-permute-start.16 = (f32[16,256]{1,0:T(8,128)S(1)}, f32[16,256]{1,0:T(8,128)S(1)}, u32[]{:S(2)}, u32[]{:S(2)}) collective-permute-start(f32[16,256]{1,0:T(8,128)S(1)} %dynamic-slice_add_fusion.3), channel_id=1, source_target_pairs={{0,4},{1,5},{2,6},{3,7},{4,8},{5,9},{6,10},{7,11},{8,12},{9,13},{1... | collective-permute-start | bytes 49160 | tf_op jit(solution)/shard_map/reduce_weight/ppermute | solution.py:31
  151.4 4.2 %collective-permute-start.21 = (f32[16,256]{1,0:T(8,128)S(1)}, f32[16,256]{1,0:T(8,128)S(1)}, u32[]{:S(2)}, u32[]{:S(2)}) collective-permute-start(f32[16,256]{1,0:T(8,128)S(1)} %fusion.8), channel_id=1, source_target_pairs={{0,3},{1,0},{2,1},{3,2},{4,7},{5,4},{6,5},{7,6},{8,11},{9,8},{10,9... | collective-permute-start | bytes 49160 | tf_op jit(solution)/shard_map/reduce_weight/ppermute | solution.py:31
  153.5 4.6 %collective-permute-start.20 = (f32[16,256]{1,0:T(8,128)S(1)}, f32[16,256]{1,0:T(8,128)S(1)}, u32[]{:S(2)}, u32[]{:S(2)}) collective-permute-start(f32[16,256]{1,0:T(8,128)S(1)} %fusion.8), channel_id=1, source_target_pairs={{0,2},{1,3},{2,0},{3,1},{4,6},{5,7},{6,4},{7,5},{8,10},{9,11},{10,... | collective-permute-start | bytes 49160 | tf_op jit(solution)/shard_map/reduce_weight/ppermute | solution.py:31
  153.7 5.5 %collective-permute-start.19 = (f32[16,256]{1,0:T(8,128)S(1)}, f32[16,256]{1,0:T(8,128)S(1)}, u32[]{:S(2)}, u32[]{:S(2)}) collective-permute-start(f32[16,256]{1,0:T(8,128)S(1)} %fusion.8), channel_id=1, source_target_pairs={{0,1},{1,2},{2,3},{3,0},{4,5},{5,6},{6,7},{7,4},{8,9},{9,10},{10,1... | collective-permute-start | bytes 49160 | tf_op jit(solution)/shard_map/reduce_weight/ppermute | solution.py:31
  159.2 7.7 %collective-permute-start.22 = (f32[16,256]{1,0:T(8,128)S(1)}, f32[16,256]{1,0:T(8,128)S(1)}, u32[]{:S(2)}, u32[]{:S(2)}) collective-permute-start(f32[16,256]{1,0:T(8,128)S(1)} %fusion.7), channel_id=1, source_target_pairs={{0,128},{16,144},{32,160},{48,176},{64,192},{80,208},{96,224},{112... | collective-permute-start | bytes 49160 | tf_op jit(solution)/shard_map/reduce_weight/ppermute | solution.py:24
  167.0 9.7 %collective-permute-start.25 = (f32[32,256]{1,0:T(8,128)S(1)}, f32[32,256]{1,0:T(8,128)S(1)}, u32[]{:S(2)}, u32[]{:S(2)}) collective-permute-start(f32[32,256]{1,0:T(8,128)S(1)} %bitcast.57), channel_id=1, source_target_pairs={{0,96},{16,112},{32,0},{48,16},{64,32},{80,48},{96,64},{112,80},{1... | collective-permute-start | bytes 98312 | tf_op jit(solution)/shard_map/reduce_weight/ppermute | solution.py:24
  168.0 8.8 %collective-permute-start.24 = (f32[32,256]{1,0:T(8,128)S(1)}, f32[32,256]{1,0:T(8,128)S(1)}, u32[]{:S(2)}, u32[]{:S(2)}) collective-permute-start(f32[32,256]{1,0:T(8,128)S(1)} %bitcast.58), channel_id=1, source_target_pairs={{0,64},{16,80},{32,96},{48,112},{64,0},{80,16},{96,32},{112,48},{1... | collective-permute-start | bytes 98312 | tf_op jit(solution)/shard_map/reduce_weight/ppermute | solution.py:24
  170.5 6.3 %collective-permute-start.23 = (f32[32,256]{1,0:T(8,128)S(1)}, f32[32,256]{1,0:T(8,128)S(1)}, u32[]{:S(2)}, u32[]{:S(2)}) collective-permute-start(f32[32,256]{1,0:T(8,128)S(1)} %bitcast.59), channel_id=1, source_target_pairs={{0,32},{16,48},{32,64},{48,80},{64,96},{80,112},{96,0},{112,16},{1... | collective-permute-start | bytes 98312 | tf_op jit(solution)/shard_map/reduce_weight/ppermute | solution.py:24
  173.4 8.8 %collective-permute-start.34 = (bf16[2,256,256]{2,1,0:T(8,128)(2,1)S(1)}, bf16[2,256,256]{2,1,0:T(8,128)(2,1)S(1)}, u32[]{:S(2)}, u32[]{:S(2)}) collective-permute-start(bf16[2,256,256]{2,1,0:T(8,128)(2,1)S(1)} %get-tuple-element.25), channel_id=1, source_target_pairs={{0,32},{16,48},{32,64},{48,80},{64,96},{80,112},{96,0},{112,16},{1... | collective-permute-start | bytes 786440 | tf_op jit(solution)/shard_map/reduce_features/ppermute | solution.py:24
  173.5 10.1 %collective-permute-start.36 = (bf16[2,256,256]{2,1,0:T(8,128)(2,1)S(1)}, bf16[2,256,256]{2,1,0:T(8,128)(2,1)S(1)}, u32[]{:S(2)}, u32[]{:S(2)}) collective-permute-start(bf16[2,256,256]{2,1,0:T(8,128)(2,1)S(1)} %get-tuple-element.26), channel_id=1, source_target_pairs={{0,96},{16,112},{32,0},{48,16},{64,32},{80,48},{96,64},{112,80},{1... | collective-permute-start | bytes 786440 | tf_op jit(solution)/shard_map/reduce_features/ppermute | solution.py:24
  176.7 8.3 %collective-permute-start.35 = (bf16[2,256,256]{2,1,0:T(8,128)(2,1)S(1)}, bf16[2,256,256]{2,1,0:T(8,128)(2,1)S(1)}, u32[]{:S(2)}, u32[]{:S(2)}) collective-permute-start(bf16[2,256,256]{2,1,0:T(8,128)(2,1)S(1)} %get-tuple-element.27), channel_id=1, source_target_pairs={{0,64},{16,80},{32,96},{48,112},{64,0},{80,16},{96,32},{112,48},{1... | collective-permute-start | bytes 786440 | tf_op jit(solution)/shard_map/reduce_features/ppermute | solution.py:24
  176.9 14.0 %collective-permute-start.26 = (f32[128,256]{1,0:T(8,128)S(1)}, f32[128,256]{1,0:T(8,128)S(1)}, u32[]{:S(2)}, u32[]{:S(2)}) collective-permute-start(f32[128,256]{1,0:T(8,128)S(1)} %bitcast.51), channel_id=1, source_target_pairs={{0,16},{16,0},{32,48},{48,32},{64,80},{80,64},{96,112},{112,96},{1... | collective-permute-start | bytes 393224 | tf_op jit(solution)/shard_map/reduce_weight/ppermute | solution.py:24
  185.1 9.0 %collective-permute-start.37 = (bf16[256,256]{1,0:T(8,128)(2,1)S(1)}, bf16[256,256]{1,0:T(8,128)(2,1)S(1)}, u32[]{:S(2)}, u32[]{:S(2)}) collective-permute-start(bf16[256,256]{1,0:T(8,128)(2,1)S(1)} %fusion.5), channel_id=1, source_target_pairs={{0,128},{16,144},{32,160},{48,176},{64,192},{80,208},{96,224},{112... | collective-permute-start | bytes 393224 | tf_op jit(solution)/shard_map/reduce_features/ppermute | solution.py:24

commit v2 on v1

v2 whole, which is shorter than its diff:
```python
import functools
import math

import jax
import jax.numpy as jnp
from jax import lax
from jax.experimental import pallas as pl
from jax.experimental.pallas import tpu as pltpu
from jax.sharding import PartitionSpec as P

ROW_DEVICES = 16
COL_DEVICES = 16
UNROLL = 4
EDGE = 256
HALF = 128
GROUP = 4 * EDGE
WEIGHT_ROWS = 128
VMEM_BYTES = 48 << 20
BF16 = jnp.bfloat16
F32 = jnp.float32


def row_permute(value, zh=0, y=0, core=0):
    pairs = []
    for i in range(ROW_DEVICES):
        to_zh, to_y, to_core = (i >> 3) ^ zh, (((i >> 1) & 3) + y) % 4, (i & 1) ^ core
        pairs.append((i, (to_zh * 4 + to_y) * 2 + to_core))
    return lax.ppermute(value, "row", pairs)


def col_permute(value, x=0, zl=0):
    pairs = []
    for i in range(COL_DEVICES):
        pairs.append((i, (((i >> 2) + x) % 4) * 4 + ((i & 3) + zl) % 4))
    return lax.ppermute(value, "col", pairs)


def row_tile(k, j, flip):
    index = lax.axis_index("row")
    zh, y, core = index >> 3, (index >> 1) & 3, index & 1
    return ((zh ^ j) * 4 + ((y + k) & 3)) * 2 + (core ^ flip)


def col_tile(k, j):
    index = lax.axis_index("col")
    return (((index >> 2) + k) & 3) * 4 + ((index + j) & 3)


def tile_loop(count, into, frm, tiles, panel, tile_buf, acc, tile_sem, piece_copies, contract):
    @pl.loop(0, count)
    def _(i):
        pltpu.make_async_copy(tiles.at[i], tile_buf.at[i], tile_sem.at[i]).start()

    for copy in piece_copies:
        copy.start()

    @pl.loop(0, acc.shape[0])
    def _(i):
        acc[i] = jnp.zeros(acc.shape[1:], F32)

    for copy in piece_copies:
        copy.wait()

    def arrive(i):
        pltpu.make_async_copy(tiles.at[i], tile_buf.at[i], tile_sem.at[i]).wait()

    def product(i):
        return lax.dot_general(
            tile_buf[i], panel[frm[i]], (((contract,), (0,)), ((), ())), preferred_element_type=F32
        )

    groups = count // UNROLL

    @pl.loop(0, groups)
    def _(group):
        first = group * UNROLL
        for j in range(UNROLL):
            arrive(first + j)
        terms = [product(first + j) for j in range(UNROLL)]
        for j in range(UNROLL):
            acc[into[first + j]] += terms[j]

    @pl.loop(groups * UNROLL, count)
    def _(i):
        arrive(i)
        acc[into[i]] += product(i)


def forward_kernel(cnt, into, frm, near, far, tiles, o0, o1, o2, o3, panel, tile_buf, acc, tile_sem, piece_sem):
    copies = []
    for flip, piece in enumerate((near, far)):
        for k in range(4):
            for j in range(2):
                n = k * 2 + j
                copies.append(
                    pltpu.make_async_copy(
                        piece.at[n], panel.at[row_tile(-k, j, flip)], piece_sem.at[flip * 8 + n]
                    )
                )
    tile_loop(cnt[0], into, frm, tiles, panel, tile_buf, acc, tile_sem, copies, 1)
    for k, out in enumerate((o0, o1, o2, o3)):
        for j in range(4):
            out[j] = acc[col_tile(k, j)].astype(BF16)


def backward_kernel(with_weight, cnt, into, frm, g0, g1, g2, g3, tiles, *refs):
    if with_weight:
        own, sent, panel, tile_buf, acc, tile_sem, piece_sem, weight_buf = refs
    else:
        own, sent, panel, tile_buf, acc, tile_sem, piece_sem = refs
    copies = []
    for k, piece in enumerate((g0, g1, g2, g3)):
        for j in range(4):
            copies.append(
                pltpu.make_async_copy(
                    piece.at[pl.ds(j * EDGE, EDGE)], panel.at[col_tile(-k, -j)], piece_sem.at[k * 4 + j]
                )
            )
    if with_weight:
        for k, piece in enumerate((g0, g1, g2, g3)):
            copies.append(
                pltpu.make_async_copy(
                    piece.at[pl.ds(GROUP, WEIGHT_ROWS)], weight_buf.at[k], piece_sem.at[16 + k]
                )
            )
    tile_loop(cnt[0], into, frm, tiles, panel, tile_buf, acc, tile_sem, copies, 0)
    if with_weight:
        x = lax.axis_index("col") >> 2
        term = weight_buf[x].astype(F32)
        for place in range(1, 4):
            term = term + weight_buf[(x - place) & 3].astype(F32)
        term = term.astype(BF16)
    for flip, out in enumerate((own, sent)):
        for k in range(4):
            for j in range(2):
                out[k, j * EDGE : (j + 1) * EDGE] = acc[row_tile(k, j, flip)].astype(BF16)
            if with_weight:
                out[k, 2 * EDGE :] = term


def tile_call(kernel, name, cnt, into, frm, pieces, tiles, out_shapes, with_weight=False):
    slots, edge, _ = tiles.shape
    smem = pl.BlockSpec(memory_space=pltpu.SMEM)
    hbm = pl.BlockSpec(memory_space=pl.ANY)
    vmem = pl.BlockSpec(memory_space=pltpu.VMEM)
    scratch = [
        pltpu.VMEM((16, edge, HALF), BF16),
        pltpu.VMEM((slots, edge, edge), BF16),
        pltpu.VMEM((16, edge, HALF), F32),
        pltpu.SemaphoreType.DMA((slots,)),
        pltpu.SemaphoreType.DMA((20,)),
    ]
    if with_weight:
        scratch.append(pltpu.VMEM((4, WEIGHT_ROWS, HALF), BF16))
    return pl.pallas_call(
        kernel,
        out_shape=[jax.ShapeDtypeStruct(shape, BF16) for shape in out_shapes],
        in_specs=[smem] * 3 + [hbm] * (len(pieces) + 1),
        out_specs=[vmem] * len(out_shapes),
        scratch_shapes=scratch,
        compiler_params=pltpu.CompilerParams(vmem_limit_bytes=VMEM_BYTES),
        cost_estimate=pl.CostEstimate(
            flops=2 * slots * edge**3, bytes_accessed=slots * edge * edge * 2, transcendentals=0
        ),
        name=name,
    )(cnt, into, frm, *pieces, tiles)


def small_call(kernel, name, out_shapes, operands, scratch=(), flops=10**6):
    return pl.pallas_call(
        kernel,
        out_shape=[jax.ShapeDtypeStruct(shape, dtype) for shape, dtype in out_shapes],
        scratch_shapes=list(scratch),
        compiler_params=pltpu.CompilerParams(vmem_limit_bytes=8 << 20),
        cost_estimate=pl.CostEstimate(flops=flops, bytes_accessed=10**6, transcendentals=0),
        name=name,
    )(*operands)


def dense_kernel(*refs):
    quads, (weight, grad_out, activation, weight_own, m0, z1, z2, z3, m1, term) = refs[:8], refs[8:]
    aggregated = []
    for own, q1, q2, q3 in (quads[:4], quads[4:]):
        total = own[...] + q1[...].astype(F32) + q2[...].astype(F32) + q3[...].astype(F32)
        aggregated.append(total.astype(BF16))
    pre_act = jnp.dot(aggregated[0], weight[:HALF], preferred_element_type=F32)
    pre_act += jnp.dot(aggregated[1], weight[HALF:], preferred_element_type=F32)
    gate_sig = 1.0 / (1.0 + jnp.exp(-pre_act))
    activation[...] = (pre_act * gate_sig).astype(BF16)
    slope = gate_sig * (1.0 + pre_act * (1.0 - gate_sig))
    act_grad = (grad_out[...].astype(F32) * slope).astype(BF16)
    msg_grad = lax.dot_general(
        act_grad, weight[...], (((1,), (1,)), ((), ())), preferred_element_type=F32
    ).astype(BF16)
    for out in (m0, z1, z2, z3):
        out[:EDGE] = msg_grad[:, :HALF]
    m1[...] = msg_grad[:, HALF:]
    for part in range(2):
        term[part * HALF : (part + 1) * HALF] = lax.dot_general(
            aggregated[part], act_grad, (((0,), (0,)), ((), ())), preferred_element_type=F32
        )
    zl = lax.axis_index("col") & 3
    for k, (out, base) in enumerate(((weight_own, 0), (z1, EDGE), (z2, EDGE), (z3, EDGE))):
        rows = pl.ds(pl.multiple_of(((zl + k) & 3) * 64, 64), 64)
        for side in range(2):
            first = base + side * 64
            out[first : first + 64] = term[rows, side * HALF : (side + 1) * HALF].astype(out.dtype)


def dense_call(sums, weight, grad_out):
    return small_call(
        dense_kernel,
        "dense",
        [(grad_out.shape, BF16), ((HALF, HALF), F32), ((EDGE, HALF), BF16)]
        + [((EDGE + HALF, HALF), BF16)] * 3
        + [((EDGE, HALF), BF16)],
        (*sums, weight, grad_out),
        [pltpu.VMEM((EDGE, EDGE), F32)],
        6 * 256**3,
    )


def pack_kernel(m0, z1, z2, z3, weight_own, group):
    term = weight_own[...]
    for piece in (z1, z2, z3):
        term = term + piece[EDGE:].astype(F32)
    for j, piece in enumerate((m0, z1, z2, z3)):
        group[j * EDGE : (j + 1) * EDGE] = piece[:EDGE]
    group[GROUP:] = term.astype(BF16)


def pack_call(m0, received, weight_own):
    return small_call(
        pack_kernel,
        "pack_messages",
        [((GROUP + WEIGHT_ROWS, HALF), BF16)],
        (m0, *received, weight_own),
    )[0]


def add_y_kernel(q0, q1, q2, q3, kept, given, buf):
    quads = (q0, q1, q2, q3)
    total = quads[0][...].astype(F32)
    for quad in quads[1:]:
        total = total + quad[...].astype(F32)
    kept[...] = total[:EDGE]
    given[:EDGE] = total[EDGE : 2 * EDGE].astype(BF16)
    if given.shape[0] > EDGE:
        for k, quad in enumerate(quads):
            buf[k] = quad[2 * EDGE :].astype(F32)
        y = (lax.axis_index("row") >> 1) & 3
        term = buf[y]
        for place in range(1, 4):
            term = term + buf[(y - place) & 3]
        given[EDGE:] = term.astype(BF16)


def add_y_call(quads):
    rows = quads[0].shape[0]
    return small_call(
        add_y_kernel,
        "add_over_y",
        [((EDGE, HALF), F32), ((rows - EDGE, HALF), BF16)],
        quads,
        [pltpu.VMEM((4, WEIGHT_ROWS, HALF), F32)],
    )


def spread_kernel(scale, a0, a1, a2, a3, out):
    col = lax.axis_index("col")
    for k, piece in enumerate((a0, a1, a2, a3)):
        row = pl.multiple_of(((col - k) & 3) * 64, 64)
        for side in range(2):
            out[pl.ds(row, 64), side * HALF : (side + 1) * HALF] = piece[side * 64 : side * 64 + 64] * scale


def add_all(pieces):
    total = pieces[0].astype(F32)
    for piece in pieces[1:]:
        total = total + piece.astype(F32)
    return total


def local(features, adj_tiles, tile_rows, tile_cols, tile_count, weight, grad_out):
    tiles = adj_tiles[0, 0]
    row_ids, col_ids, count = tile_rows[0, 0], tile_cols[0, 0], tile_count[0]
    node_total = EDGE * ROW_DEVICES * COL_DEVICES

    with jax.named_scope("gather_features"):
        other = row_permute(features, zh=1)
        pairs = [
            jnp.stack([value[:, h * HALF : (h + 1) * HALF] for value in (features, other)]) for h in range(2)
        ]
    for h in range(2):
        with jax.named_scope("gather_features"):
            near = jnp.concatenate([pairs[h]] + [row_permute(pairs[h], y=k) for k in (1, 2, 3)])
            if h == 1:
                near, before = lax.optimization_barrier((near, parts))
            far = row_permute(near, core=1)
            if h == 0:
                far, pairs[1] = lax.optimization_barrier((far, pairs[1]))
        parts = tile_call(
            forward_kernel, "forward_tiles", count, row_ids, col_ids, [near, far], tiles, [(4, EDGE, HALF)] * 4
        )
    sums = []
    for parts in (before, parts):
        with jax.named_scope("reduce_aggregate"):
            parts = [parts[0]] + [col_permute(parts[k], x=k) for k in (1, 2, 3)]
            part_sums = [add_all([part[j] for part in parts]) for j in range(4)]
            sums += [part_sums[0]] + [col_permute(part_sums[k].astype(BF16), zl=k) for k in (1, 2, 3)]

    activation, weight_own, m0, z1, z2, z3, m1 = dense_call(sums, weight, grad_out)

    with jax.named_scope("gather_messages"):
        arrived = [col_permute(z, zl=k) for k, z in ((1, z1), (2, z2), (3, z3))]
        group = pack_call(m0, arrived, weight_own)
        first = [group] + [col_permute(group, x=k) for k in (1, 2, 3)]
        group = jnp.concatenate([m1] + [col_permute(m1, zl=k) for k in (1, 2, 3)])
        first, group = lax.optimization_barrier((first, group))
        second = [group] + [col_permute(group, x=k) for k in (1, 2, 3)]

    kept, given = [None, None], [None, None]
    for h, group in enumerate((first, second)):
        if h == 1:
            group, given[0] = lax.optimization_barrier((group, given[0]))
        rows = 2 * EDGE + (WEIGHT_ROWS if h == 0 else 0)
        own, sent = tile_call(
            functools.partial(backward_kernel, h == 0),
            "backward_tiles",
            count,
            col_ids,
            row_ids,
            group,
            tiles,
            [(4, rows, HALF)] * 2,
            h == 0,
        )
        if h == 1:
            with jax.named_scope("reduce_features"):
                first = row_permute(given[0], zh=1)
            own, sent, first = lax.optimization_barrier((own, sent, first))
        with jax.named_scope("reduce_features"):
            both = add_all([own, row_permute(sent, core=1)]).astype(BF16)
            quads = [both[0]] + [row_permute(both[k], y=k) for k in (1, 2, 3)]
            kept[h], given[h] = add_y_call(quads)
    with jax.named_scope("reduce_features"):
        last = [first, row_permute(given[1], zh=1)]
        halves = [mine + theirs[:EDGE].astype(F32) for mine, theirs in zip(kept, last)]
    with jax.named_scope("gather_weight"):
        mine = given[0][EDGE:].astype(F32) + last[0][EDGE:].astype(F32)
        mine = [mine] + [col_permute(mine, zl=k) for k in (1, 2, 3)]
    x_grad = jnp.concatenate(halves, axis=1).astype(BF16)
    weight_grad = small_call(
        functools.partial(spread_kernel, 1.0 / math.sqrt(node_total)), "spread_weight", [((EDGE, EDGE), F32)], mine
    )[0]

    return (activation, weight_grad, x_grad)


def solution(mesh):
    return jax.shard_map(
        local,
        mesh=mesh,
        in_specs=(
            P(("col", "row"), None),
            P("row", "col", None, None, None),
            P("row", "col", None),
            P("row", "col", None),
            P("row", "col"),
            P(),
            P(("row", "col"), None),
        ),
        out_specs=(P(("row", "col"), None), P(), P(("col", "row"), None)),
        check_vma=False,
    )
```

time: 197 us -> 168 us (0.85)
  waiting for transfers between devices: 89.3 us -> 49.2 us
  Pallas kernels: 15.8 us -> 27.6 us
  starting transfers between devices: 75.6 us -> 85.5 us
  other arithmetic: 7.97 us -> 1.42 us
  local copies, waits for them, and re-layouts: 4.45 us -> 1.91 us
    ppermute x18 -> x27, waiting for transfers between devices: 52.2 us -> 27.7 us  [col_permute(): return lax.ppermute(value, 'col', pairs)]
    ppermute x18 -> x27, starting transfers between devices: 35.3 us -> 52.9 us  [col_permute(): return lax.ppermute(value, 'col', pairs)]
    ppermute x20 -> x19, waiting for transfers between devices: 37.2 us -> 21.5 us  [row_permute(): return lax.ppermute(value, 'row', pairs)]
    pallas_call x2 -> x4, Pallas kernels: 13.4 us -> 25.6 us  [tile_call(): pl.pallas_call(kernel, out_shape=[jax.ShapeDtypeStruct(shape, BF16) for s...]
    ppermute x20 -> x19, starting transfers between devices: 40.3 us -> 32.6 us  [row_permute(): return lax.ppermute(value, 'row', pairs)]
    unnamed x22 -> x12, local copies, waits for them, and re-layouts: 3.41 us -> 0.92 us
  transfers between devices with their start and end apart: 38 -> 46, of which waited for: 22 -> 22; matrix products, arithmetic and copies ran while one was open for 3% -> 1% of each run, Pallas kernels for 3% -> 12%
where the time goes in v2:
time: 168 us; the launch traced here: 167 us
  starting transfers between devices  85.5 us (51%)
  waiting for transfers between devices  49.2 us (29%)
  Pallas kernels  27.6 us (16%)
  local copies, waits for them, and re-layouts  1.91 us (1%)
    ppermute x27, starting transfers between devices, col_permute(): return lax.ppermute(value, 'col', pairs)  52.9 us
    ppermute x19, starting transfers between devices, row_permute(): return lax.ppermute(value, 'row', pairs)  32.6 us
    ppermute x27, waiting for transfers between devices, col_permute(): return lax.ppermute(value, 'col', pairs)  27.7 us
    pallas_call x4, Pallas kernels, tile_call(): pl.pallas_call(kernel, out_shape=[jax.ShapeDtypeStruct(shape, BF16) for s...  25.6 us
    ppermute x19, waiting for transfers between devices, row_permute(): return lax.ppermute(value, 'row', pairs)  21.5 us
  transfers between devices with their start and end apart: 46, of which 22 were waited for; matrix products, arithmetic and copies ran while one was open for 1% of the time, Pallas kernels for 12%

profile of v2, /device:TPU:2, one launch (start us, length us, event | category | flops | bytes accessed | tf_op | source)
XLA Modules:
  0.0 167.2 jit_solution(16845900221144805111)
XLA Ops:
  0.7 7.3 %collective-permute-start = (bf16[256,256]{1,0:T(8,128)(2,1)}, bf16[256,256]{1,0:T(8,128)(2,1)S(1)}, u32[]{:S(2)}, u32[]{:S(2)}) collective-permute-start(bf16[256,256]{1,0:T(8,128)(2,1)} %param.7), channel_id=1, source_target_pairs={{0,128},{16,144},{32,160},{48,176},{64,192},{80,208},{96,224},{112... | collective-permute-start | bytes 393224 | tf_op jit(solution)/shard_map/gather_features/ppermute | solution.py:28
  7.9 0.9 slice_bitcast_fusion.10
  8.8 0.8 constant_dynamic-update-slice_fusion.4
  9.7 2.1 %collective-permute-done = bf16[256,256]{1,0:T(8,128)(2,1)S(1)} collective-permute-done((bf16[256,256]{1,0:T(8,128)(2,1)}, bf16[256,256]{1,0:T(8,128)(2,1)S(1)}, u32[]{:S(2)}, u32[]{:S(2)}) %collective-permute-start) | collective-permute-done | bytes 131104 | tf_op jit(solution)/shard_map/gather_features/ppermute | solution.py:28
  11.8 1.7 collective-permute-start.1
  13.4 2.9 %collective-permute-start.2 = (bf16[2,256,128]{2,1,0:T(8,128)(2,1)S(1)}, bf16[2,256,128]{2,1,0:T(8,128)(2,1)S(1)}, u32[]{:S(2)}, u32[]{:S(2)}) collective-permute-start(bf16[2,256,128]{2,1,0:T(8,128)(2,1)S(1)} %pad_maximum_fusion.2), channel_id=1, source_target_pairs={{0,64},{16,80},{32,96},{48,112},{64,0},{80,16},{96,32},{112,48},{1... | collective-permute-start | bytes 393224 | tf_op jit(solution)/shard_map/gather_features/ppermute | solution.py:28
  16.3 1.3 collective-permute-start.3
  17.7 1.3 collective-permute-done.1
  19.1 2.6 %collective-permute-done.2 = bf16[2,256,128]{2,1,0:T(8,128)(2,1)S(1)} collective-permute-done((bf16[2,256,128]{2,1,0:T(8,128)(2,1)S(1)}, bf16[2,256,128]{2,1,0:T(8,128)(2,1)S(1)}, u32[]{:S(2)}, u32[]{:S(2)}) %collective-permute-start.2) | collective-permute-done | bytes 131104 | tf_op jit(solution)/shard_map/gather_features/ppermute | solution.py:28
  22.5 1.2 collective-permute-done.4.far
  23.8 1.2 collective-permute-start.5
  25.0 2.8 %collective-permute-start.6 = (bf16[2,256,128]{2,1,0:T(8,128)(2,1)S(1)}, bf16[2,256,128]{2,1,0:T(8,128)(2,1)S(1)}, u32[]{:S(2)}, u32[]{:S(2)}) collective-permute-start(bf16[2,256,128]{2,1,0:T(8,128)(2,1)S(1)} %pad_maximum_fusion.3), channel_id=1, source_target_pairs={{0,64},{16,80},{32,96},{48,112},{64,0},{80,16},{96,32},{112,48},{1... | collective-permute-start | bytes 393224 | tf_op jit(solution)/shard_map/gather_features/ppermute | solution.py:28
  27.8 1.1 collective-permute-start.7
  28.9 6.1 %forward_tiles.2 = (bf16[4,256,128]{2,1,0:T(8,128)(2,1)S(1)}, bf16[4,256,128]{2,1,0:T(8,128)(2,1)S(1)}, bf16[4,256,128]{2,1,0:T(8,128)(2,1)S(1)}, bf16[4,256,128]{2,1,0:T(8,128)(2,1)S(1)}) custom-call(s32[1]{0:T(128)} %bitcast.48.cnt, s32[80]{0:T(128)S(1)} %bitcast.52, s32[80]{0:T(128)S(1)} %bitcast.56, ...), custom_call_target="tpu_custom_call" | custom-call | flops 2684354560 | bytes 10485760 | tf_op jit(solution)/shard_map/forward_tiles/pallas_call | solution.py:155
  35.3 1.1 collective-permute-start.10
  36.4 3.2 %collective-permute-start.8 = (bf16[4,256,128]{2,1,0:T(8,128)(2,1)S(1)}, bf16[4,256,128]{2,1,0:T(8,128)(2,1)S(1)}, u32[]{:S(2)}, u32[]{:S(2)}) collective-permute-start(bf16[4,256,128]{2,1,0:T(8,128)(2,1)S(1)} %get-tuple-element.53), channel_id=1, source_target_pairs={{0,4},{1,5},{2,6},{3,7},{4,8},{5,9},{6,10},{7,11},{8,12},{9,13},{1... | collective-permute-start | bytes 786440 | tf_op jit(solution)/shard_map/reduce_aggregate/ppermute | solution.py:35
  39.6 1.5 collective-permute-start.9
  41.0 6.1 %forward_tiles.3 = (bf16[4,256,128]{2,1,0:T(8,128)(2,1)S(1)}, bf16[4,256,128]{2,1,0:T(8,128)(2,1)S(1)}, bf16[4,256,128]{2,1,0:T(8,128)(2,1)S(1)}, bf16[4,256,128]{2,1,0:T(8,128)(2,1)S(1)}) custom-call(s32[1]{0:T(128)} %bitcast.49.cnt, s32[80]{0:T(128)S(1)} %bitcast.53, s32[80]{0:T(128)S(1)} %bitcast.57, bf16[8,256,128]{2,1,0:T(8,128)(2,1)S(1)} %pad_maximum_fusion.near, ...), custom_call_target="tpu_custom_call" | custom-call | flops 2684354560 | bytes 10485760 | tf_op jit(solution)/shard_map/forward_tiles/pallas_call | solution.py:155
  47.3 5.2 %collective-permute-start.16 = (bf16[4,256,128]{2,1,0:T(8,128)(2,1)S(1)}, bf16[4,256,128]{2,1,0:T(8,128)(2,1)S(1)}, u32[]{:S(2)}, u32[]{:S(2)}) collective-permute-start(bf16[4,256,128]{2,1,0:T(8,128)(2,1)S(1)} %get-tuple-element.59), channel_id=1, source_target_pairs={{0,8},{1,9},{2,10},{3,11},{4,12},{5,13},{6,14},{7,15},{8,0},{9,1},... | collective-permute-start | bytes 786440 | tf_op jit(solution)/shard_map/reduce_aggregate/ppermute | solution.py:35
  53.1 2.9 %collective-permute-start.11 = (bf16[256,128]{1,0:T(8,128)(2,1)S(1)}, bf16[256,128]{1,0:T(8,128)(2,1)S(1)}, u32[]{:S(2)}, u32[]{:S(2)}) collective-permute-start(bf16[256,128]{1,0:T(8,128)(2,1)S(1)} %get-tuple-element.95), channel_id=1, source_target_pairs={{0,1},{1,2},{2,3},{3,0},{4,5},{5,6},{6,7},{7,4},{8,9},{9,10},{10,1... | collective-permute-start | bytes 196616 | tf_op jit(solution)/shard_map/reduce_aggregate/ppermute | solution.py:35
  56.6 5.4 %collective-permute-done.15 = bf16[4,256,128]{2,1,0:T(8,128)(2,1)S(1)} collective-permute-done((bf16[4,256,128]{2,1,0:T(8,128)(2,1)S(1)}, bf16[4,256,128]{2,1,0:T(8,128)(2,1)S(1)}, u32[]{:S(2)}, u32[]{:S(2)}) %collective-permute-start.15) | collective-permute-done | bytes 262176 | tf_op jit(solution)/shard_map/reduce_aggregate/ppermute | solution.py:35
  62.0 2.8 %collective-permute-done.17 = bf16[4,256,128]{2,1,0:T(8,128)(2,1)S(1)} collective-permute-done((bf16[4,256,128]{2,1,0:T(8,128)(2,1)S(1)}, bf16[4,256,128]{2,1,0:T(8,128)(2,1)S(1)}, u32[]{:S(2)}, u32[]{:S(2)}) %collective-permute-start.17) | collective-permute-done | bytes 262176 | tf_op jit(solution)/shard_map/reduce_aggregate/ppermute | solution.py:35
  65.0 1.6 collective-permute-start.18
  66.6 1.9 %collective-permute-start.19 = (bf16[256,128]{1,0:T(8,128)(2,1)S(1)}, bf16[256,128]{1,0:T(8,128)(2,1)S(1)}, u32[]{:S(2)}, u32[]{:S(2)}) collective-permute-start(bf16[256,128]{1,0:T(8,128)(2,1)S(1)} %get-tuple-element.90), channel_id=1, source_target_pairs={{0,2},{1,3},{2,0},{3,1},{4,6},{5,7},{6,4},{7,5},{8,10},{9,11},{10,... | collective-permute-start | bytes 196616 | tf_op jit(solution)/shard_map/reduce_aggregate/ppermute | solution.py:35
  68.5 1.9 %collective-permute-start.20 = (bf16[256,128]{1,0:T(8,128)(2,1)S(1)}, bf16[256,128]{1,0:T(8,128)(2,1)S(1)}, u32[]{:S(2)}, u32[]{:S(2)}) collective-permute-start(bf16[256,128]{1,0:T(8,128)(2,1)S(1)} %get-tuple-element.89), channel_id=1, source_target_pairs={{0,3},{1,0},{2,1},{3,2},{4,7},{5,4},{6,5},{7,6},{8,11},{9,8},{10,9... | collective-permute-start | bytes 196616 | tf_op jit(solution)/shard_map/reduce_aggregate/ppermute | solution.py:35
  70.4 1.3 collective-permute-done.18.refs_5_
  71.7 2.3 %collective-permute-done.19.refs_6_ = bf16[256,128]{1,0:T(8,128)(2,1)S(1)} collective-permute-done((bf16[256,128]{1,0:T(8,128)(2,1)S(1)}, bf16[256,128]{1,0:T(8,128)(2,1)S(1)}, u32[]{:S(2)}, u32[]{:S(2)}) %collective-permute-start.19) | collective-permute-done | bytes 65568 | tf_op jit(solution)/shard_map/reduce_aggregate/ppermute | solution.py:35
  74.1 1.0 dense.1
  75.1 1.3 collective-permute-start.21
  76.3 1.9 %collective-permute-start.22 = (bf16[384,128]{1,0:T(8,128)(2,1)S(1)}, bf16[384,128]{1,0:T(8,128)(2,1)S(1)}, u32[]{:S(2)}, u32[]{:S(2)}) collective-permute-start(bf16[384,128]{1,0:T(8,128)(2,1)S(1)} %get-tuple-element.64), channel_id=1, source_target_pairs={{0,2},{1,3},{2,0},{3,1},{4,6},{5,7},{6,4},{7,5},{8,10},{9,11},{10,... | collective-permute-start | bytes 294920 | tf_op jit(solution)/shard_map/gather_messages/ppermute | solution.py:35
  78.2 0.7 collective-permute-start.23
  78.9 3.1 %collective-permute-done.21.z1 = bf16[384,128]{1,0:T(8,128)(2,1)S(1)} collective-permute-done((bf16[384,128]{1,0:T(8,128)(2,1)S(1)}, bf16[384,128]{1,0:T(8,128)(2,1)S(1)}, u32[]{:S(2)}, u32[]{:S(2)}) %collective-permute-start.21) | collective-permute-done | bytes 98336 | tf_op jit(solution)/shard_map/gather_messages/ppermute | solution.py:35
  82.0 2.7 %collective-permute-done.22.z2 = bf16[384,128]{1,0:T(8,128)(2,1)S(1)} collective-permute-done((bf16[384,128]{1,0:T(8,128)(2,1)S(1)}, bf16[384,128]{1,0:T(8,128)(2,1)S(1)}, u32[]{:S(2)}, u32[]{:S(2)}) %collective-permute-start.22) | collective-permute-done | bytes 98336 | tf_op jit(solution)/shard_map/gather_messages/ppermute | solution.py:35
  84.7 2.0 %collective-permute-start.24 = (bf16[1152,128]{1,0:T(8,128)(2,1)S(1)}, bf16[1152,128]{1,0:T(8,128)(2,1)S(1)}, u32[]{:S(2)}, u32[]{:S(2)}) collective-permute-start(bf16[1152,128]{1,0:T(8,128)(2,1)S(1)} %pack_messages.1.g0), channel_id=1, source_target_pairs={{0,4},{1,5},{2,6},{3,7},{4,8},{5,9},{6,10},{7,11},{8,12},{9,13},{1... | collective-permute-start | bytes 884744 | tf_op jit(solution)/shard_map/gather_messages/ppermute | solution.py:35
  86.7 2.8 %collective-permute-start.25 = (bf16[1152,128]{1,0:T(8,128)(2,1)S(1)}, bf16[1152,128]{1,0:T(8,128)(2,1)S(1)}, u32[]{:S(2)}, u32[]{:S(2)}) collective-permute-start(bf16[1152,128]{1,0:T(8,128)(2,1)S(1)} %pack_messages.1.g0), channel_id=1, source_target_pairs={{0,8},{1,9},{2,10},{3,11},{4,12},{5,13},{6,14},{7,15},{8,0},{9,1},... | collective-permute-start | bytes 884744 | tf_op jit(solution)/shard_map/gather_messages/ppermute | solution.py:35
  89.5 0.7 collective-permute-start.26
  90.2 2.6 %collective-permute-start.27 = (bf16[256,128]{1,0:T(8,128)(2,1)S(1)}, bf16[256,128]{1,0:T(8,128)(2,1)S(1)}, u32[]{:S(2)}, u32[]{:S(2)}) collective-permute-start(bf16[256,128]{1,0:T(8,128)(2,1)S(1)} %get-tuple-element.67), channel_id=1, source_target_pairs={{0,1},{1,2},{2,3},{3,0},{4,5},{5,6},{6,7},{7,4},{8,9},{9,10},{10,1... | collective-permute-start | bytes 196616 | tf_op jit(solution)/shard_map/gather_messages/ppermute | solution.py:35
  92.7 0.8 collective-permute-start.28
  93.5 2.8 %collective-permute-done.27 = bf16[256,128]{1,0:T(8,128)(2,1)S(1)} collective-permute-done((bf16[256,128]{1,0:T(8,128)(2,1)S(1)}, bf16[256,128]{1,0:T(8,128)(2,1)S(1)}, u32[]{:S(2)}, u32[]{:S(2)}) %collective-permute-start.27) | collective-permute-done | bytes 65568 | tf_op jit(solution)/shard_map/gather_messages/ppermute | solution.py:35
  96.4 1.2 collective-permute-start.29
  97.5 1.4 collective-permute-done.28
  98.9 1.7 %collective-permute-done.29 = bf16[256,128]{1,0:T(8,128)(2,1)S(1)} collective-permute-done((bf16[256,128]{1,0:T(8,128)(2,1)S(1)}, bf16[256,128]{1,0:T(8,128)(2,1)S(1)}, u32[]{:S(2)}, u32[]{:S(2)}) %collective-permute-start.29) | collective-permute-done | bytes 65568 | tf_op jit(solution)/shard_map/gather_messages/ppermute | solution.py:35
  101.1 6.8 %backward_tiles.2 = (bf16[4,640,128]{2,1,0:T(8,128)(2,1)S(1)}, bf16[4,640,128]{2,1,0:T(8,128)(2,1)S(1)}) custom-call(s32[1]{0:T(128)} %bitcast.50.cnt, s32[80]{0:T(128)S(1)} %bitcast.58, s32[80]{0:T(128)S(1)} %bitcast.54, bf16[1152,128]{1,0:T(8,128)(2,1)S(1)} %pack_messages.1.g0, bf16[1152,128]{1,0:T(8,128)(2,1)S(1)} %collective-permute-done.24.g1, ...), custom_call_target="tpu_custom_call" | custom-call | flops 2684354560 | bytes 10485760 | tf_op jit(solution)/shard_map/backward_tiles/pallas_call | solution.py:155
  108.2 2.1 %collective-permute-done.33 = bf16[4,640,128]{2,1,0:T(8,128)(2,1)S(1)} collective-permute-done((bf16[4,640,128]{2,1,0:T(8,128)(2,1)S(1)}, bf16[4,640,128]{2,1,0:T(8,128)(2,1)S(1)}, u32[]{:S(2)}, u32[]{:S(2)}) %collective-permute-start.33) | collective-permute-done | bytes 655392 | tf_op jit(solution)/shard_map/reduce_features/ppermute | solution.py:28
  110.5 1.2 collective-permute-start.34
  111.7 1.3 collective-permute-start.30
  113.0 5.7 %collective-permute-start.31 = (bf16[1024,128]{1,0:T(8,128)(2,1)S(1)}, bf16[1024,128]{1,0:T(8,128)(2,1)S(1)}, u32[]{:S(2)}, u32[]{:S(2)}) collective-permute-start(bf16[1024,128]{1,0:T(8,128)(2,1)S(1)} %pad_maximum_fusion.1.g0), channel_id=1, source_target_pairs={{0,8},{1,9},{2,10},{3,11},{4,12},{5,13},{6,14},{7,15},{8,0},{9,1},... | collective-permute-start | bytes 786440 | tf_op jit(solution)/shard_map/gather_messages/ppermute | solution.py:35
  118.7 2.6 %collective-permute-start.32 = (bf16[1024,128]{1,0:T(8,128)(2,1)S(1)}, bf16[1024,128]{1,0:T(8,128)(2,1)S(1)}, u32[]{:S(2)}, u32[]{:S(2)}) collective-permute-start(bf16[1024,128]{1,0:T(8,128)(2,1)S(1)} %pad_maximum_fusion.1.g0), channel_id=1, source_target_pairs={{0,12},{1,13},{2,14},{3,15},{4,0},{5,1},{6,2},{7,3},{8,4},{9,5},{1... | collective-permute-start | bytes 786440 | tf_op jit(solution)/shard_map/gather_messages/ppermute | solution.py:35
  122.0 2.5 %collective-permute-start.36 = (bf16[640,128]{1,0:T(8,128)(2,1)S(1)}, bf16[640,128]{1,0:T(8,128)(2,1)S(1)}, u32[]{:S(2)}, u32[]{:S(2)}) collective-permute-start(bf16[640,128]{1,0:T(8,128)(2,1)S(1)} %get-tuple-element.97), channel_id=1, source_target_pairs={{0,96},{16,112},{32,0},{48,16},{64,32},{80,48},{96,64},{112,80},{1... | collective-permute-start | bytes 491528 | tf_op jit(solution)/shard_map/reduce_features/ppermute | solution.py:28
  124.5 3.6 %collective-permute-done.35.q2 = bf16[640,128]{1,0:T(8,128)(2,1)S(1)} collective-permute-done((bf16[640,128]{1,0:T(8,128)(2,1)S(1)}, bf16[640,128]{1,0:T(8,128)(2,1)S(1)}, u32[]{:S(2)}, u32[]{:S(2)}) %collective-permute-start.35) | collective-permute-done | bytes 163872 | tf_op jit(solution)/shard_map/reduce_features/ppermute | solution.py:28
  128.2 0.8 collective-permute-done.36.q3
  129.1 1.7 %collective-permute-done.32.g3 = bf16[1024,128]{1,0:T(8,128)(2,1)S(1)} collective-permute-done((bf16[1024,128]{1,0:T(8,128)(2,1)S(1)}, bf16[1024,128]{1,0:T(8,128)(2,1)S(1)}, u32[]{:S(2)}, u32[]{:S(2)}) %collective-permute-start.32) | collective-permute-done | bytes 262176 | tf_op jit(solution)/shard_map/gather_messages/ppermute | solution.py:35
  130.8 2.1 %collective-permute-start.37 = (bf16[384,128]{1,0:T(8,128)(2,1)S(1)}, bf16[384,128]{1,0:T(8,128)(2,1)S(1)}, u32[]{:S(2)}, u32[]{:S(2)}) collective-permute-start(bf16[384,128]{1,0:T(8,128)(2,1)S(1)} %get-tuple-element.76), channel_id=1, source_target_pairs={{0,128},{16,144},{32,160},{48,176},{64,192},{80,208},{96,224},{112... | collective-permute-start | bytes 294920 | tf_op jit(solution)/shard_map/reduce_features/ppermute | solution.py:28
  132.9 6.6 %backward_tiles.3 = (bf16[4,512,128]{2,1,0:T(8,128)(2,1)S(1)}, bf16[4,512,128]{2,1,0:T(8,128)(2,1)S(1)}) custom-call(s32[1]{0:T(128)} %bitcast.51.cnt, s32[80]{0:T(128)S(1)} %bitcast.59, s32[80]{0:T(128)S(1)} %bitcast.55, bf16[1024,128]{1,0:T(8,128)(2,1)S(1)} %pad_maximum_fusion.1.g0, bf16[1024,128]{1,0:T(8,128)(2,1)S(1)} %collective-permute-done.30.g1, ...), custom_call_target="tpu_custom_call" | custom-call | flops 2684354560 | bytes 10485760 | tf_op jit(solution)/shard_map/backward_tiles/pallas_call | solution.py:155
  139.6 1.9 %collective-permute-done.41 = bf16[4,512,128]{2,1,0:T(8,128)(2,1)S(1)} collective-permute-done((bf16[4,512,128]{2,1,0:T(8,128)(2,1)S(1)}, bf16[4,512,128]{2,1,0:T(8,128)(2,1)S(1)}, u32[]{:S(2)}, u32[]{:S(2)}) %collective-permute-start.41) | collective-permute-done | bytes 524320 | tf_op jit(solution)/shard_map/reduce_features/ppermute | solution.py:28
  141.7 0.8 collective-permute-start.42
  142.6 4.5 %collective-permute-start.43 = (bf16[512,128]{1,0:T(8,128)(2,1)S(1)}, bf16[512,128]{1,0:T(8,128)(2,1)S(1)}, u32[]{:S(2)}, u32[]{:S(2)}) collective-permute-start(bf16[512,128]{1,0:T(8,128)(2,1)S(1)} %get-tuple-element.102), channel_id=1, source_target_pairs={{0,64},{16,80},{32,96},{48,112},{64,0},{80,16},{96,32},{112,48},{1... | collective-permute-start | bytes 393224 | tf_op jit(solution)/shard_map/reduce_features/ppermute | solution.py:28
  147.1 1.6 collective-permute-start.44
  148.6 3.4 %collective-permute-start.38 = (f32[128,128]{1,0:T(8,128)S(1)}, f32[128,128]{1,0:T(8,128)S(1)}, u32[]{:S(2)}, u32[]{:S(2)}) collective-permute-start(f32[128,128]{1,0:T(8,128)S(1)} %convert_add_fusion.a0), channel_id=1, source_target_pairs={{0,1},{1,2},{2,3},{3,0},{4,5},{5,6},{6,7},{7,4},{8,9},{9,10},{10,1... | collective-permute-start | bytes 196616 | tf_op jit(solution)/shard_map/gather_weight/ppermute | solution.py:35
  152.0 0.7 collective-permute-start.39
  152.8 5.4 %collective-permute-start.40 = (f32[128,128]{1,0:T(8,128)S(1)}, f32[128,128]{1,0:T(8,128)S(1)}, u32[]{:S(2)}, u32[]{:S(2)}) collective-permute-start(f32[128,128]{1,0:T(8,128)S(1)} %convert_add_fusion.a0), channel_id=1, source_target_pairs={{0,3},{1,0},{2,1},{3,2},{4,7},{5,4},{6,5},{7,6},{8,11},{9,8},{10,9... | collective-permute-start | bytes 196616 | tf_op jit(solution)/shard_map/gather_weight/ppermute | solution.py:35
  158.6 1.5 collective-permute-done.40.a3
  160.1 0.7 spread_weight.1
  160.8 5.7 %collective-permute-done.45 = bf16[256,128]{1,0:T(8,128)(2,1)S(1)} collective-permute-done((bf16[256,128]{1,0:T(8,128)(2,1)S(1)}, bf16[256,128]{1,0:T(8,128)(2,1)S(1)}, u32[]{:S(2)}, u32[]{:S(2)}) %collective-permute-start.45) | collective-permute-done | bytes 65568 | tf_op jit(solution)/shard_map/reduce_features/ppermute | solution.py:28
  (66 shorter events, 5.0 us)
Async XLA Ops:
  0.6 28.3 %copy-start.2 = (s32[1,1,80]{2,1,0:T(1,128)S(1)}, s32[1,1,80]{2,1,0:T(1,128)}, u32[]{:S(2)}) copy-start(s32[1,1,80]{2,1,0:T(1,128)} %param.9) | copy-start | bytes 964
  0.6 28.3 %copy-start.3 = (s32[1,1,80]{2,1,0:T(1,128)S(1)}, s32[1,1,80]{2,1,0:T(1,128)}, u32[]{:S(2)}) copy-start(s32[1,1,80]{2,1,0:T(1,128)} %param.10) | copy-start | bytes 964
  0.7 11.1 %collective-permute-start = (bf16[256,256]{1,0:T(8,128)(2,1)}, bf16[256,256]{1,0:T(8,128)(2,1)S(1)}, u32[]{:S(2)}, u32[]{:S(2)}) collective-permute-start(bf16[256,256]{1,0:T(8,128)(2,1)} %param.7), channel_id=1, source_target_pairs={{0,128},{16,144},{32,160},{48,176},{64,192},{80,208},{96,224},{112... | collective-permute-start | bytes 393224 | tf_op jit(solution)/shard_map/gather_features/ppermute | solution.py:28
  11.8 7.3 %collective-permute-start.1 = (bf16[2,256,128]{2,1,0:T(8,128)(2,1)S(1)}, bf16[2,256,128]{2,1,0:T(8,128)(2,1)S(1)}, u32[]{:S(2)}, u32[]{:S(2)}) collective-permute-start(bf16[2,256,128]{2,1,0:T(8,128)(2,1)S(1)} %pad_maximum_fusion.2), channel_id=1, source_target_pairs={{0,32},{16,48},{32,64},{48,80},{64,96},{80,112},{96,0},{112,16},{1... | collective-permute-start | bytes 393224 | tf_op jit(solution)/shard_map/gather_features/ppermute | solution.py:28
  13.4 8.3 %collective-permute-start.2 = (bf16[2,256,128]{2,1,0:T(8,128)(2,1)S(1)}, bf16[2,256,128]{2,1,0:T(8,128)(2,1)S(1)}, u32[]{:S(2)}, u32[]{:S(2)}) collective-permute-start(bf16[2,256,128]{2,1,0:T(8,128)(2,1)S(1)} %pad_maximum_fusion.2), channel_id=1, source_target_pairs={{0,64},{16,80},{32,96},{48,112},{64,0},{80,16},{96,32},{112,48},{1... | collective-permute-start | bytes 393224 | tf_op jit(solution)/shard_map/gather_features/ppermute | solution.py:28
  16.3 5.4 %collective-permute-start.3 = (bf16[2,256,128]{2,1,0:T(8,128)(2,1)S(1)}, bf16[2,256,128]{2,1,0:T(8,128)(2,1)S(1)}, u32[]{:S(2)}, u32[]{:S(2)}) collective-permute-start(bf16[2,256,128]{2,1,0:T(8,128)(2,1)S(1)} %pad_maximum_fusion.2), channel_id=1, source_target_pairs={{0,96},{16,112},{32,0},{48,16},{64,32},{80,48},{96,64},{112,80},{1... | collective-permute-start | bytes 393224 | tf_op jit(solution)/shard_map/gather_features/ppermute | solution.py:28
  21.8 2.0 %collective-permute-start.4 = (bf16[8,256,128]{2,1,0:T(8,128)(2,1)S(1)}, bf16[8,256,128]{2,1,0:T(8,128)(2,1)S(1)}, u32[]{:S(2)}, u32[]{:S(2)}) collective-permute-start(bf16[8,256,128]{2,1,0:T(8,128)(2,1)S(1)} %constant_dynamic-update-slice_fusion.near), channel_id=1, source_target_pairs={{0,16},{16,0},{32,48},{48,32},{64,80},{80,64},{96,112},{112,96},{1... | collective-permute-start | bytes 1572872 | tf_op jit(solution)/shard_map/gather_features/ppermute | solution.py:28
  23.8 11.3 %collective-permute-start.5 = (bf16[2,256,128]{2,1,0:T(8,128)(2,1)S(1)}, bf16[2,256,128]{2,1,0:T(8,128)(2,1)S(1)}, u32[]{:S(2)}, u32[]{:S(2)}) collective-permute-start(bf16[2,256,128]{2,1,0:T(8,128)(2,1)S(1)} %pad_maximum_fusion.3), channel_id=1, source_target_pairs={{0,32},{16,48},{32,64},{48,80},{64,96},{80,112},{96,0},{112,16},{1... | collective-permute-start | bytes 393224 | tf_op jit(solution)/shard_map/gather_features/ppermute | solution.py:28
  25.0 10.1 %collective-permute-start.6 = (bf16[2,256,128]{2,1,0:T(8,128)(2,1)S(1)}, bf16[2,256,128]{2,1,0:T(8,128)(2,1)S(1)}, u32[]{:S(2)}, u32[]{:S(2)}) collective-permute-start(bf16[2,256,128]{2,1,0:T(8,128)(2,1)S(1)} %pad_maximum_fusion.3), channel_id=1, source_target_pairs={{0,64},{16,80},{32,96},{48,112},{64,0},{80,16},{96,32},{112,48},{1... | collective-permute-start | bytes 393224 | tf_op jit(solution)/shard_map/gather_features/ppermute | solution.py:28
  27.8 7.3 %collective-permute-start.7 = (bf16[2,256,128]{2,1,0:T(8,128)(2,1)S(1)}, bf16[2,256,128]{2,1,0:T(8,128)(2,1)S(1)}, u32[]{:S(2)}, u32[]{:S(2)}) collective-permute-start(bf16[2,256,128]{2,1,0:T(8,128)(2,1)S(1)} %pad_maximum_fusion.3), channel_id=1, source_target_pairs={{0,96},{16,112},{32,0},{48,16},{64,32},{80,48},{96,64},{112,80},{1... | collective-permute-start | bytes 393224 | tf_op jit(solution)/shard_map/gather_features/ppermute | solution.py:28
  35.2 5.9 %collective-permute-start.14 = (bf16[8,256,128]{2,1,0:T(8,128)(2,1)S(1)}, bf16[8,256,128]{2,1,0:T(8,128)(2,1)S(1)}, u32[]{:S(2)}, u32[]{:S(2)}) collective-permute-start(bf16[8,256,128]{2,1,0:T(8,128)(2,1)S(1)} %pad_maximum_fusion.near), channel_id=1, source_target_pairs={{0,16},{16,0},{32,48},{48,32},{64,80},{80,64},{96,112},{112,96},{1... | collective-permute-start | bytes 1572872 | tf_op jit(solution)/shard_map/gather_features/ppermute | solution.py:28
  35.3 17.2 %collective-permute-start.10 = (bf16[4,256,128]{2,1,0:T(8,128)(2,1)S(1)}, bf16[4,256,128]{2,1,0:T(8,128)(2,1)S(1)}, u32[]{:S(2)}, u32[]{:S(2)}) collective-permute-start(bf16[4,256,128]{2,1,0:T(8,128)(2,1)S(1)} %get-tuple-element.55), channel_id=1, source_target_pairs={{0,12},{1,13},{2,14},{3,15},{4,0},{5,1},{6,2},{7,3},{8,4},{9,5},{1... | collective-permute-start | bytes 786440 | tf_op jit(solution)/shard_map/reduce_aggregate/ppermute | solution.py:35
  36.4 16.1 %collective-permute-start.8 = (bf16[4,256,128]{2,1,0:T(8,128)(2,1)S(1)}, bf16[4,256,128]{2,1,0:T(8,128)(2,1)S(1)}, u32[]{:S(2)}, u32[]{:S(2)}) collective-permute-start(bf16[4,256,128]{2,1,0:T(8,128)(2,1)S(1)} %get-tuple-element.53), channel_id=1, source_target_pairs={{0,4},{1,5},{2,6},{3,7},{4,8},{5,9},{6,10},{7,11},{8,12},{9,13},{1... | collective-permute-start | bytes 786440 | tf_op jit(solution)/shard_map/reduce_aggregate/ppermute | solution.py:35
  39.6 13.4 %collective-permute-start.9 = (bf16[4,256,128]{2,1,0:T(8,128)(2,1)S(1)}, bf16[4,256,128]{2,1,0:T(8,128)(2,1)S(1)}, u32[]{:S(2)}, u32[]{:S(2)}) collective-permute-start(bf16[4,256,128]{2,1,0:T(8,128)(2,1)S(1)} %get-tuple-element.54), channel_id=1, source_target_pairs={{0,8},{1,9},{2,10},{3,11},{4,12},{5,13},{6,14},{7,15},{8,0},{9,1},... | collective-permute-start | bytes 786440 | tf_op jit(solution)/shard_map/reduce_aggregate/ppermute | solution.py:35
  47.2 14.8 %collective-permute-start.15 = (bf16[4,256,128]{2,1,0:T(8,128)(2,1)S(1)}, bf16[4,256,128]{2,1,0:T(8,128)(2,1)S(1)}, u32[]{:S(2)}, u32[]{:S(2)}) collective-permute-start(bf16[4,256,128]{2,1,0:T(8,128)(2,1)S(1)} %get-tuple-element.58), channel_id=1, source_target_pairs={{0,4},{1,5},{2,6},{3,7},{4,8},{5,9},{6,10},{7,11},{8,12},{9,13},{1... | collective-permute-start | bytes 786440 | tf_op jit(solution)/shard_map/reduce_aggregate/ppermute | solution.py:35
  47.3 14.8 %collective-permute-start.16 = (bf16[4,256,128]{2,1,0:T(8,128)(2,1)S(1)}, bf16[4,256,128]{2,1,0:T(8,128)(2,1)S(1)}, u32[]{:S(2)}, u32[]{:S(2)}) collective-permute-start(bf16[4,256,128]{2,1,0:T(8,128)(2,1)S(1)} %get-tuple-element.59), channel_id=1, source_target_pairs={{0,8},{1,9},{2,10},{3,11},{4,12},{5,13},{6,14},{7,15},{8,0},{9,1},... | collective-permute-start | bytes 786440 | tf_op jit(solution)/shard_map/reduce_aggregate/ppermute | solution.py:35
  52.5 21.6 %copy-start = (bf16[256,256]{1,0:T(8,128)(2,1)S(1)}, bf16[256,256]{1,0:T(8,128)(2,1)}, u32[]{:S(2)}) copy-start(bf16[256,256]{1,0:T(8,128)(2,1)} %refs_8_.1) | copy-start | bytes 393220
  52.5 21.6 %copy-start.1 = (bf16[256,256]{1,0:T(8,128)(2,1)S(1)}, bf16[256,256]{1,0:T(8,128)(2,1)}, u32[]{:S(2)}) copy-start(bf16[256,256]{1,0:T(8,128)(2,1)} %refs_9_.1) | copy-start | bytes 393220
  52.5 12.4 %collective-permute-start.17 = (bf16[4,256,128]{2,1,0:T(8,128)(2,1)S(1)}, bf16[4,256,128]{2,1,0:T(8,128)(2,1)S(1)}, u32[]{:S(2)}, u32[]{:S(2)}) collective-permute-start(bf16[4,256,128]{2,1,0:T(8,128)(2,1)S(1)} %get-tuple-element.60), channel_id=1, source_target_pairs={{0,12},{1,13},{2,14},{3,15},{4,0},{5,1},{6,2},{7,3},{8,4},{9,5},{1... | collective-permute-start | bytes 786440 | tf_op jit(solution)/shard_map/reduce_aggregate/ppermute | solution.py:35
  53.1 15.5 %collective-permute-start.11 = (bf16[256,128]{1,0:T(8,128)(2,1)S(1)}, bf16[256,128]{1,0:T(8,128)(2,1)S(1)}, u32[]{:S(2)}, u32[]{:S(2)}) collective-permute-start(bf16[256,128]{1,0:T(8,128)(2,1)S(1)} %get-tuple-element.95), channel_id=1, source_target_pairs={{0,1},{1,2},{2,3},{3,0},{4,5},{5,6},{6,7},{7,4},{8,9},{9,10},{10,1... | collective-permute-start | bytes 196616 | tf_op jit(solution)/shard_map/reduce_aggregate/ppermute | solution.py:35
  56.0 14.4 %collective-permute-start.12 = (bf16[256,128]{1,0:T(8,128)(2,1)S(1)}, bf16[256,128]{1,0:T(8,128)(2,1)S(1)}, u32[]{:S(2)}, u32[]{:S(2)}) collective-permute-start(bf16[256,128]{1,0:T(8,128)(2,1)S(1)} %get-tuple-element.94), channel_id=1, source_target_pairs={{0,2},{1,3},{2,0},{3,1},{4,6},{5,7},{6,4},{7,5},{8,10},{9,11},{10,... | collective-permute-start | bytes 196616 | tf_op jit(solution)/shard_map/reduce_aggregate/ppermute | solution.py:35
  62.0 8.4 %collective-permute-start.13 = (bf16[256,128]{1,0:T(8,128)(2,1)S(1)}, bf16[256,128]{1,0:T(8,128)(2,1)S(1)}, u32[]{:S(2)}, u32[]{:S(2)}) collective-permute-start(bf16[256,128]{1,0:T(8,128)(2,1)S(1)} %get-tuple-element.93), channel_id=1, source_target_pairs={{0,3},{1,0},{2,1},{3,2},{4,7},{5,4},{6,5},{7,6},{8,11},{9,8},{10,9... | collective-permute-start | bytes 196616 | tf_op jit(solution)/shard_map/reduce_aggregate/ppermute | solution.py:35
  65.0 6.7 %collective-permute-start.18 = (bf16[256,128]{1,0:T(8,128)(2,1)S(1)}, bf16[256,128]{1,0:T(8,128)(2,1)S(1)}, u32[]{:S(2)}, u32[]{:S(2)}) collective-permute-start(bf16[256,128]{1,0:T(8,128)(2,1)S(1)} %get-tuple-element.91), channel_id=1, source_target_pairs={{0,1},{1,2},{2,3},{3,0},{4,5},{5,6},{6,7},{7,4},{8,9},{9,10},{10,1... | collective-permute-start | bytes 196616 | tf_op jit(solution)/shard_map/reduce_aggregate/ppermute | solution.py:35
  66.6 7.5 %collective-permute-start.19 = (bf16[256,128]{1,0:T(8,128)(2,1)S(1)}, bf16[256,128]{1,0:T(8,128)(2,1)S(1)}, u32[]{:S(2)}, u32[]{:S(2)}) collective-permute-start(bf16[256,128]{1,0:T(8,128)(2,1)S(1)} %get-tuple-element.90), channel_id=1, source_target_pairs={{0,2},{1,3},{2,0},{3,1},{4,6},{5,7},{6,4},{7,5},{8,10},{9,11},{10,... | collective-permute-start | bytes 196616 | tf_op jit(solution)/shard_map/reduce_aggregate/ppermute | solution.py:35
  68.5 5.5 %collective-permute-start.20 = (bf16[256,128]{1,0:T(8,128)(2,1)S(1)}, bf16[256,128]{1,0:T(8,128)(2,1)S(1)}, u32[]{:S(2)}, u32[]{:S(2)}) collective-permute-start(bf16[256,128]{1,0:T(8,128)(2,1)S(1)} %get-tuple-element.89), channel_id=1, source_target_pairs={{0,3},{1,0},{2,1},{3,2},{4,7},{5,4},{6,5},{7,6},{8,11},{9,8},{10,9... | collective-permute-start | bytes 196616 | tf_op jit(solution)/shard_map/reduce_aggregate/ppermute | solution.py:35
  75.1 6.9 %collective-permute-start.21 = (bf16[384,128]{1,0:T(8,128)(2,1)S(1)}, bf16[384,128]{1,0:T(8,128)(2,1)S(1)}, u32[]{:S(2)}, u32[]{:S(2)}) collective-permute-start(bf16[384,128]{1,0:T(8,128)(2,1)S(1)} %get-tuple-element.63), channel_id=1, source_target_pairs={{0,1},{1,2},{2,3},{3,0},{4,5},{5,6},{6,7},{7,4},{8,9},{9,10},{10,1... | collective-permute-start | bytes 294920 | tf_op jit(solution)/shard_map/gather_messages/ppermute | solution.py:35
  76.3 8.4 %collective-permute-start.22 = (bf16[384,128]{1,0:T(8,128)(2,1)S(1)}, bf16[384,128]{1,0:T(8,128)(2,1)S(1)}, u32[]{:S(2)}, u32[]{:S(2)}) collective-permute-start(bf16[384,128]{1,0:T(8,128)(2,1)S(1)} %get-tuple-element.64), channel_id=1, source_target_pairs={{0,2},{1,3},{2,0},{3,1},{4,6},{5,7},{6,4},{7,5},{8,10},{9,11},{10,... | collective-permute-start | bytes 294920 | tf_op jit(solution)/shard_map/gather_messages/ppermute | solution.py:35
  78.2 6.5 %collective-permute-start.23 = (bf16[384,128]{1,0:T(8,128)(2,1)S(1)}, bf16[384,128]{1,0:T(8,128)(2,1)S(1)}, u32[]{:S(2)}, u32[]{:S(2)}) collective-permute-start(bf16[384,128]{1,0:T(8,128)(2,1)S(1)} %get-tuple-element.65), channel_id=1, source_target_pairs={{0,3},{1,0},{2,1},{3,2},{4,7},{5,4},{6,5},{7,6},{8,11},{9,8},{10,9... | collective-permute-start | bytes 294920 | tf_op jit(solution)/shard_map/gather_messages/ppermute | solution.py:35
  84.7 15.9 %collective-permute-start.24 = (bf16[1152,128]{1,0:T(8,128)(2,1)S(1)}, bf16[1152,128]{1,0:T(8,128)(2,1)S(1)}, u32[]{:S(2)}, u32[]{:S(2)}) collective-permute-start(bf16[1152,128]{1,0:T(8,128)(2,1)S(1)} %pack_messages.1.g0), channel_id=1, source_target_pairs={{0,4},{1,5},{2,6},{3,7},{4,8},{5,9},{6,10},{7,11},{8,12},{9,13},{1... | collective-permute-start | bytes 884744 | tf_op jit(solution)/shard_map/gather_messages/ppermute | solution.py:35
  86.7 14.0 %collective-permute-start.25 = (bf16[1152,128]{1,0:T(8,128)(2,1)S(1)}, bf16[1152,128]{1,0:T(8,128)(2,1)S(1)}, u32[]{:S(2)}, u32[]{:S(2)}) collective-permute-start(bf16[1152,128]{1,0:T(8,128)(2,1)S(1)} %pack_messages.1.g0), channel_id=1, source_target_pairs={{0,8},{1,9},{2,10},{3,11},{4,12},{5,13},{6,14},{7,15},{8,0},{9,1},... | collective-permute-start | bytes 884744 | tf_op jit(solution)/shard_map/gather_messages/ppermute | solution.py:35
  89.5 11.6 %collective-permute-start.26 = (bf16[1152,128]{1,0:T(8,128)(2,1)S(1)}, bf16[1152,128]{1,0:T(8,128)(2,1)S(1)}, u32[]{:S(2)}, u32[]{:S(2)}) collective-permute-start(bf16[1152,128]{1,0:T(8,128)(2,1)S(1)} %pack_messages.1.g0), channel_id=1, source_target_pairs={{0,12},{1,13},{2,14},{3,15},{4,0},{5,1},{6,2},{7,3},{8,4},{9,5},{1... | collective-permute-start | bytes 884744 | tf_op jit(solution)/shard_map/gather_messages/ppermute | solution.py:35
  90.2 6.2 %collective-permute-start.27 = (bf16[256,128]{1,0:T(8,128)(2,1)S(1)}, bf16[256,128]{1,0:T(8,128)(2,1)S(1)}, u32[]{:S(2)}, u32[]{:S(2)}) collective-permute-start(bf16[256,128]{1,0:T(8,128)(2,1)S(1)} %get-tuple-element.67), channel_id=1, source_target_pairs={{0,1},{1,2},{2,3},{3,0},{4,5},{5,6},{6,7},{7,4},{8,9},{9,10},{10,1... | collective-permute-start | bytes 196616 | tf_op jit(solution)/shard_map/gather_messages/ppermute | solution.py:35
  92.7 6.2 %collective-permute-start.28 = (bf16[256,128]{1,0:T(8,128)(2,1)S(1)}, bf16[256,128]{1,0:T(8,128)(2,1)S(1)}, u32[]{:S(2)}, u32[]{:S(2)}) collective-permute-start(bf16[256,128]{1,0:T(8,128)(2,1)S(1)} %get-tuple-element.67), channel_id=1, source_target_pairs={{0,2},{1,3},{2,0},{3,1},{4,6},{5,7},{6,4},{7,5},{8,10},{9,11},{10,... | collective-permute-start | bytes 196616 | tf_op jit(solution)/shard_map/gather_messages/ppermute | solution.py:35
  96.4 4.3 %collective-permute-start.29 = (bf16[256,128]{1,0:T(8,128)(2,1)S(1)}, bf16[256,128]{1,0:T(8,128)(2,1)S(1)}, u32[]{:S(2)}, u32[]{:S(2)}) collective-permute-start(bf16[256,128]{1,0:T(8,128)(2,1)S(1)} %get-tuple-element.67), channel_id=1, source_target_pairs={{0,3},{1,0},{2,1},{3,2},{4,7},{5,4},{6,5},{7,6},{8,11},{9,8},{10,9... | collective-permute-start | bytes 196616 | tf_op jit(solution)/shard_map/gather_messages/ppermute | solution.py:35
  107.8 2.4 %collective-permute-start.33 = (bf16[4,640,128]{2,1,0:T(8,128)(2,1)S(1)}, bf16[4,640,128]{2,1,0:T(8,128)(2,1)S(1)}, u32[]{:S(2)}, u32[]{:S(2)}) collective-permute-start(bf16[4,640,128]{2,1,0:T(8,128)(2,1)S(1)} %get-tuple-element.74), channel_id=1, source_target_pairs={{0,16},{16,0},{32,48},{48,32},{64,80},{80,64},{96,112},{112,96},{1... | collective-permute-start | bytes 1966088 | tf_op jit(solution)/shard_map/reduce_features/ppermute | solution.py:28
  110.5 11.5 %collective-permute-start.34 = (bf16[640,128]{1,0:T(8,128)(2,1)S(1)}, bf16[640,128]{1,0:T(8,128)(2,1)S(1)}, u32[]{:S(2)}, u32[]{:S(2)}) collective-permute-start(bf16[640,128]{1,0:T(8,128)(2,1)S(1)} %get-tuple-element.99), channel_id=1, source_target_pairs={{0,32},{16,48},{32,64},{48,80},{64,96},{80,112},{96,0},{112,16},{1... | collective-permute-start | bytes 491528 | tf_op jit(solution)/shard_map/reduce_features/ppermute | solution.py:28
  111.7 17.4 %collective-permute-start.30 = (bf16[1024,128]{1,0:T(8,128)(2,1)S(1)}, bf16[1024,128]{1,0:T(8,128)(2,1)S(1)}, u32[]{:S(2)}, u32[]{:S(2)}) collective-permute-start(bf16[1024,128]{1,0:T(8,128)(2,1)S(1)} %pad_maximum_fusion.1.g0), channel_id=1, source_target_pairs={{0,4},{1,5},{2,6},{3,7},{4,8},{5,9},{6,10},{7,11},{8,12},{9,13},{1... | collective-permute-start | bytes 786440 | tf_op jit(solution)/shard_map/gather_messages/ppermute | solution.py:35
  113.0 16.1 %collective-permute-start.31 = (bf16[1024,128]{1,0:T(8,128)(2,1)S(1)}, bf16[1024,128]{1,0:T(8,128)(2,1)S(1)}, u32[]{:S(2)}, u32[]{:S(2)}) collective-permute-start(bf16[1024,128]{1,0:T(8,128)(2,1)S(1)} %pad_maximum_fusion.1.g0), channel_id=1, source_target_pairs={{0,8},{1,9},{2,10},{3,11},{4,12},{5,13},{6,14},{7,15},{8,0},{9,1},... | collective-permute-start | bytes 786440 | tf_op jit(solution)/shard_map/gather_messages/ppermute | solution.py:35
  118.7 12.2 %collective-permute-start.32 = (bf16[1024,128]{1,0:T(8,128)(2,1)S(1)}, bf16[1024,128]{1,0:T(8,128)(2,1)S(1)}, u32[]{:S(2)}, u32[]{:S(2)}) collective-permute-start(bf16[1024,128]{1,0:T(8,128)(2,1)S(1)} %pad_maximum_fusion.1.g0), channel_id=1, source_target_pairs={{0,12},{1,13},{2,14},{3,15},{4,0},{5,1},{6,2},{7,3},{8,4},{9,5},{1... | collective-permute-start | bytes 786440 | tf_op jit(solution)/shard_map/gather_messages/ppermute | solution.py:35
  121.3 6.8 %collective-permute-start.35 = (bf16[640,128]{1,0:T(8,128)(2,1)S(1)}, bf16[640,128]{1,0:T(8,128)(2,1)S(1)}, u32[]{:S(2)}, u32[]{:S(2)}) collective-permute-start(bf16[640,128]{1,0:T(8,128)(2,1)S(1)} %get-tuple-element.98), channel_id=1, source_target_pairs={{0,64},{16,80},{32,96},{48,112},{64,0},{80,16},{96,32},{112,48},{1... | collective-permute-start | bytes 491528 | tf_op jit(solution)/shard_map/reduce_features/ppermute | solution.py:28
  122.0 7.0 %collective-permute-start.36 = (bf16[640,128]{1,0:T(8,128)(2,1)S(1)}, bf16[640,128]{1,0:T(8,128)(2,1)S(1)}, u32[]{:S(2)}, u32[]{:S(2)}) collective-permute-start(bf16[640,128]{1,0:T(8,128)(2,1)S(1)} %get-tuple-element.97), channel_id=1, source_target_pairs={{0,96},{16,112},{32,0},{48,16},{64,32},{80,48},{96,64},{112,80},{1... | collective-permute-start | bytes 491528 | tf_op jit(solution)/shard_map/reduce_features/ppermute | solution.py:28
  130.8 8.7 %collective-permute-start.37 = (bf16[384,128]{1,0:T(8,128)(2,1)S(1)}, bf16[384,128]{1,0:T(8,128)(2,1)S(1)}, u32[]{:S(2)}, u32[]{:S(2)}) collective-permute-start(bf16[384,128]{1,0:T(8,128)(2,1)S(1)} %get-tuple-element.76), channel_id=1, source_target_pairs={{0,128},{16,144},{32,160},{48,176},{64,192},{80,208},{96,224},{112... | collective-permute-start | bytes 294920 | tf_op jit(solution)/shard_map/reduce_features/ppermute | solution.py:28
  139.6 2.0 %collective-permute-start.41 = (bf16[4,512,128]{2,1,0:T(8,128)(2,1)S(1)}, bf16[4,512,128]{2,1,0:T(8,128)(2,1)S(1)}, u32[]{:S(2)}, u32[]{:S(2)}) collective-permute-start(bf16[4,512,128]{2,1,0:T(8,128)(2,1)S(1)} %get-tuple-element.86), channel_id=1, source_target_pairs={{0,16},{16,0},{32,48},{48,32},{64,80},{80,64},{96,112},{112,96},{1... | collective-permute-start | bytes 1572872 | tf_op jit(solution)/shard_map/reduce_features/ppermute | solution.py:28
  141.7 11.0 %collective-permute-start.42 = (bf16[512,128]{1,0:T(8,128)(2,1)S(1)}, bf16[512,128]{1,0:T(8,128)(2,1)S(1)}, u32[]{:S(2)}, u32[]{:S(2)}) collective-permute-start(bf16[512,128]{1,0:T(8,128)(2,1)S(1)} %get-tuple-element.103), channel_id=1, source_target_pairs={{0,32},{16,48},{32,64},{48,80},{64,96},{80,112},{96,0},{112,16},{1... | collective-permute-start | bytes 393224 | tf_op jit(solution)/shard_map/reduce_features/ppermute | solution.py:28
  142.6 15.6 %collective-permute-start.43 = (bf16[512,128]{1,0:T(8,128)(2,1)S(1)}, bf16[512,128]{1,0:T(8,128)(2,1)S(1)}, u32[]{:S(2)}, u32[]{:S(2)}) collective-permute-start(bf16[512,128]{1,0:T(8,128)(2,1)S(1)} %get-tuple-element.102), channel_id=1, source_target_pairs={{0,64},{16,80},{32,96},{48,112},{64,0},{80,16},{96,32},{112,48},{1... | collective-permute-start | bytes 393224 | tf_op jit(solution)/shard_map/reduce_features/ppermute | solution.py:28
  147.1 11.1 %collective-permute-start.44 = (bf16[512,128]{1,0:T(8,128)(2,1)S(1)}, bf16[512,128]{1,0:T(8,128)(2,1)S(1)}, u32[]{:S(2)}, u32[]{:S(2)}) collective-permute-start(bf16[512,128]{1,0:T(8,128)(2,1)S(1)} %get-tuple-element.101), channel_id=1, source_target_pairs={{0,96},{16,112},{32,0},{48,16},{64,32},{80,48},{96,64},{112,80},{1... | collective-permute-start | bytes 393224 | tf_op jit(solution)/shard_map/reduce_features/ppermute | solution.py:28
  148.6 9.9 %collective-permute-start.38 = (f32[128,128]{1,0:T(8,128)S(1)}, f32[128,128]{1,0:T(8,128)S(1)}, u32[]{:S(2)}, u32[]{:S(2)}) collective-permute-start(f32[128,128]{1,0:T(8,128)S(1)} %convert_add_fusion.a0), channel_id=1, source_target_pairs={{0,1},{1,2},{2,3},{3,0},{4,5},{5,6},{6,7},{7,4},{8,9},{9,10},{10,1... | collective-permute-start | bytes 196616 | tf_op jit(solution)/shard_map/gather_weight/ppermute | solution.py:35
  152.0 6.5 %collective-permute-start.39 = (f32[128,128]{1,0:T(8,128)S(1)}, f32[128,128]{1,0:T(8,128)S(1)}, u32[]{:S(2)}, u32[]{:S(2)}) collective-permute-start(f32[128,128]{1,0:T(8,128)S(1)} %convert_add_fusion.a0), channel_id=1, source_target_pairs={{0,2},{1,3},{2,0},{3,1},{4,6},{5,7},{6,4},{7,5},{8,10},{9,11},{10,... | collective-permute-start | bytes 196616 | tf_op jit(solution)/shard_map/gather_weight/ppermute | solution.py:35
  152.8 7.3 %collective-permute-start.40 = (f32[128,128]{1,0:T(8,128)S(1)}, f32[128,128]{1,0:T(8,128)S(1)}, u32[]{:S(2)}, u32[]{:S(2)}) collective-permute-start(f32[128,128]{1,0:T(8,128)S(1)} %convert_add_fusion.a0), channel_id=1, source_target_pairs={{0,3},{1,0},{2,1},{3,2},{4,7},{5,4},{6,5},{7,6},{8,11},{9,8},{10,9... | collective-permute-start | bytes 196616 | tf_op jit(solution)/shard_map/gather_weight/ppermute | solution.py:35
  158.2 8.3 %collective-permute-start.45 = (bf16[256,128]{1,0:T(8,128)(2,1)S(1)}, bf16[256,128]{1,0:T(8,128)(2,1)S(1)}, u32[]{:S(2)}, u32[]{:S(2)}) collective-permute-start(bf16[256,128]{1,0:T(8,128)(2,1)S(1)} %get-tuple-element.88), channel_id=1, source_target_pairs={{0,128},{16,144},{32,160},{48,176},{64,192},{80,208},{96,224},{112... | collective-permute-start | bytes 196616 | tf_op jit(solution)/shard_map/reduce_features/ppermute | solution.py:28
